TPU v7x, 512 devices: a whole 4x8x8 slice. The times are simulated.
512 devices in a mesh: dp: 64 (over z_lo, y, core), mp: 8 (over z_hi, x).
Axes of the slice: x: 4, y: 8, z: 8 (z_hi: 2, z_lo: 4; z = z_hi * 4 + z_lo), core: 2. Of those that a mesh axis runs over, the one named last changes fastest.
Arguments:
- hidden_states: bfloat16 [32768, 2560], P('dp'), may hold values from -16 to 16
- head_weight: bfloat16 [2560, 1024], P(None, 'mp'), may hold values from -1 to 1
- agent_bias: float32 [8, 1024], P(None, 'mp'), may hold values from -6 to 6
- agent_ids: int32 [32768], P('dp'), may hold values from 0 to 7
- actions: int32 [32768], P('dp'), may hold values from 0 to 1023
- rewards: float32 [32768], P('dp'), may hold values from -18 to 18
- values: float32 [32768], P('dp'), may hold values from -6 to 6
- episode_start: int32 [32768], P('dp'), may hold values 0 or 1
- prior_ratio: float32 [32768], P('dp'), may hold values from 0.5 to 2
- sample_rows: int32 [131072], P('dp'), may hold values from 0 to 32767, as said below
Outputs:
- natural_step: float32 [2560, 1024], P(None, 'mp')
Inputs may be any that keep to these rules, and one draw needn't show every extreme that they name: `sample_rows`: each aligned block of 2048 entries names rows of the matching block of 512 rows of hidden_states; a row may be named more than once.
All inputs are finite; a program needn't handle non-finite values. No bound on the sum of `episode_start` on one device may be relied on, other than what follows from the above.
Results may differ from a plain program's by a relative error of at most 0.003.
Values may be sent and summed in bfloat16 or wider, within the bound.
A program may use at most 64 MiB of HBM per device.

v0:
```python
import jax
import jax.numpy as jnp
from jax import lax
from jax.sharding import PartitionSpec as P

D = 2560
A = 1024
AGENTS = 8
SEQ_LEN = 64
ITERS = 2


GAMMA = 0.99
TRACE_DECAY = 0.95
DAMPING = 0.001
RADIUS_SHARE = 0.001


def advantages(rewards, values, episode_start):
    reward_rows = rewards.reshape(-1, SEQ_LEN)
    value_rows = values.reshape(-1, SEQ_LEN)
    start_rows = episode_start.reshape(-1, SEQ_LEN)
    episode_end = jnp.concatenate([start_rows[:, 1:], jnp.ones_like(start_rows[:, :1])], axis=1)
    continues = (1 - episode_end).astype(jnp.float32)
    value_next = jnp.concatenate([value_rows[:, 1:], jnp.zeros_like(value_rows[:, :1])], axis=1)
    temporal = reward_rows + GAMMA * continues * value_next - value_rows

    def backward(running, inputs):
        error, keeps = inputs
        updated = error + GAMMA * TRACE_DECAY * keeps * running
        return (updated, updated)

    final_state, advantage = lax.scan(
        backward,
        jnp.zeros((reward_rows.shape[0],), jnp.float32),
        (temporal.T, continues.T),
        reverse=True,
    )
    return advantage.T.reshape(-1)


def transpose_product(left, right):
    return lax.dot_general(
        left, right, (((0,), (0,)), ((), ())), preferred_element_type=jnp.float32
    )


def per_device(
    hidden_states,
    head_weight,
    agent_bias,
    agent_ids,
    actions,
    rewards,
    values,
    episode_start,
    prior_ratio,
    sample_rows,
):
    width_data = lax.axis_size("dp")
    local_actions = head_weight.shape[1]
    row_count = hidden_states.shape[0] * width_data
    samples_all = sample_rows.shape[0] * width_data
    advantage = advantages(rewards, values, episode_start)
    adv_total = lax.psum(jnp.sum(advantage), "dp")
    adv_mean = adv_total / row_count
    weight = prior_ratio * (advantage - adv_mean) / row_count
    agent_table = (agent_ids[:, None] == jnp.arange(AGENTS, dtype=jnp.int32)[None, :]).astype(
        jnp.float32
    )
    logits = jnp.dot(hidden_states, head_weight, preferred_element_type=jnp.float32)
    logits = logits + jnp.dot(agent_table, agent_bias, precision=lax.Precision.HIGHEST)
    local_peak = jnp.max(logits, axis=1)
    row_peak = lax.pmax(local_peak, "mp")
    exponent = jnp.exp(logits - row_peak[:, None])
    denominator = lax.psum(jnp.sum(exponent, axis=1), "mp")
    probs = exponent / denominator[:, None]
    action_base = lax.axis_index("mp") * local_actions
    picked = (
        actions[:, None] - action_base == jnp.arange(local_actions, dtype=jnp.int32)[None, :]
    ).astype(jnp.float32)
    logit_grad = (weight[:, None] * (picked - probs)).astype(jnp.bfloat16)
    local_rows = sample_rows - lax.axis_index("dp") * hidden_states.shape[0]
    sampled = jnp.take(hidden_states, local_rows, axis=0)
    sprobs = jnp.take(probs, local_rows, axis=0)
    grad = lax.psum(transpose_product(hidden_states, logit_grad), "dp")

    def global_dots(terms):
        return lax.psum((terms[0],), "mp")

    solution = jnp.zeros_like(grad)
    resid = grad
    direction = grad
    (resid_sq,) = global_dots((jnp.sum(resid * resid),))
    quad = jnp.float32(0.0)
    for iteration in range(ITERS):
        fisher_lifted = jnp.dot(
            sampled, direction.astype(jnp.bfloat16), preferred_element_type=jnp.float32
        )
        centre = lax.psum(jnp.sum(sprobs * fisher_lifted, axis=1), "mp")
        weighted = (sprobs * (fisher_lifted - centre[:, None])).astype(jnp.bfloat16)
        summed = lax.psum(transpose_product(sampled, weighted), "dp")
        fisher_image = summed / samples_all + DAMPING * direction
        (curvature,) = global_dots((jnp.sum(direction * fisher_image),))
        step_size = resid_sq / curvature
        solution = solution + step_size * direction
        resid = resid - step_size * fisher_image
        if iteration + 1 < ITERS:
            (resid_next,) = global_dots((jnp.sum(resid * resid),))
        quad = quad + step_size * step_size * curvature
        if iteration + 1 < ITERS:
            direction = resid + resid_next / resid_sq * direction
            resid_sq = resid_next
    natural_step = solution * jnp.sqrt(D * A * RADIUS_SHARE / quad)
    return natural_step


def solution(mesh):
    placed = (
        P("dp", None),
        P(None, "mp"),
        P(None, "mp"),
        P("dp"),
        P("dp"),
        P("dp"),
        P("dp"),
        P("dp"),
        P("dp"),
        P("dp"),
    )
    return jax.shard_map(
        per_device, mesh=mesh, in_specs=placed, out_specs=P(None, "mp"), check_vma=False
    )
```

profile of v0, /device:TPU:1, one launch (start us, length us, event | category | flops | bytes accessed | tf_op | source)
XLA Modules:
  0.0 1970.2 jit_solution(17376460393046283764)
XLA Ops:
  6.5 0.9 reshape.29
  7.4 0.1 slice.7
  7.5 0.8 reshape.27
  8.3 0.8 reshape.28
  9.0 0.1 slice.6
  9.1 0.1 copy.17
  9.2 0.1 copy.16
  9.3 4.8 while.17
  14.2 0.6 reduce_sum.72
  14.8 140.3 %psum.77 = f32[]{:T(128)} all-reduce(f32[]{:T(128)} %reduce_sum.72), channel_id=1, replica_groups=mesh['dp'=64,'mp'=8] {'dp'}, use_global_device_ids=true, to_apply=%region_3.4 | all-reduce | flops 1 | bytes 8 | tf_op jit(solution)/shard_map/psum | solution.py:65
  155.7 0.1 copy.18
  155.8 0.1 sub.77
  155.9 2.1 fusion.23
  158.0 0.0 copy-start.5
  158.0 0.0 copy-start.4
  158.1 0.4 fusion.22
  158.5 26.7 %pmax.7 = f32[512]{0:T(512)S(1)} all-reduce(f32[512]{0:T(512)S(1)} %get-tuple-element.146), channel_id=1, replica_groups=mesh['dp'=64,'mp'=8] {'mp'}, use_global_device_ids=true, to_apply=%region_5.6 | all-reduce | flops 512 | bytes 4096 | tf_op jit(solution)/shard_map/pmax | solution.py:74
  185.2 0.1 fusion.15
  185.2 20.5 %psum.78 = f32[512]{0:T(512)S(1)} all-reduce(f32[512]{0:T(512)S(1)} %fusion.15), channel_id=1, replica_groups=mesh['dp'=64,'mp'=8] {'mp'}, use_global_device_ids=true, to_apply=%region_7.8 | all-reduce | flops 512 | bytes 4096 | tf_op jit(solution)/shard_map/psum | solution.py:76
  205.7 0.1 fusion.14
  205.8 1.6 convolution_bitcast_fusion
  207.4 0.0 all-reduce.7.cloned.1.call-update
  207.4 0.0 all-reduce.9.cloned.1.call-start
  207.5 0.1 copy.19
  207.6 0.5 copy-done.1
  208.1 11.5 gather_fusion
  219.6 7.5 gather_fusion.1
  227.1 2.6 copy.20
  229.7 505.0 %all-reduce.7.cloned.1.call-done = f32[2560,128]{0,1:T(8,128)} async-done(((f32[2560,128]{0,1:T(8,128)}), f32[2560,128]{0,1:T(8,128)}) %all-reduce.7.cloned.1.call-update) | async-done | bytes 1310736 | tf_op jit(solution)/shard_map/psum | solution.py:86
  734.7 9.3 multiply_reduce_fusion.5
  743.9 27.5 %psum.81 = f32[2048]{0:T(1024)S(1)} all-reduce(f32[2048]{0:T(1024)S(1)} %get-tuple-element.148), channel_id=1, replica_groups=mesh['dp'=64,'mp'=8] {'mp'}, use_global_device_ids=true, to_apply=%region_12.13 | all-reduce | flops 2048 | bytes 16384 | tf_op jit(solution)/shard_map/psum | solution.py:100
  771.4 7.6 fusion.6
  779.0 0.0 all-reduce.9.cloned.1.call-update
  779.0 0.0 all-reduce.11.cloned.1.call-start
  779.1 520.4 %all-reduce.9.cloned.1.call-done = f32[2560,128]{0,1:T(8,128)} async-done(((f32[2560,128]{0,1:T(8,128)}), f32[2560,128]{0,1:T(8,128)}) %all-reduce.9.cloned.1.call-update) | async-done | bytes 1310736 | tf_op jit(solution)/shard_map/psum | solution.py:102
  1299.5 2.7 multiply_reduce_fusion.2
  1302.2 27.9 %all-reduce.2 = (f32[]{:T(128)}, f32[]{:T(128)}) all-reduce(f32[]{:T(128)} %get-tuple-element.133, f32[]{:T(128)} %get-tuple-element.132), channel_id=1, replica_groups=mesh['dp'=64,'mp'=8] {'mp'}, use_global_device_ids=true, to_apply=%region_10.11 | all-reduce | flops 2 | bytes 16 | tf_op jit(solution)/shard_map/psum | solution.py:89
  1331.4 2.7 multiply_reduce_fusion.1
  1334.1 21.0 %psum.84 = f32[]{:T(128)} all-reduce(f32[]{:T(128)} %multiply_reduce_fusion.1), channel_id=1, replica_groups=mesh['dp'=64,'mp'=8] {'mp'}, use_global_device_ids=true, to_apply=%region_17.18 | all-reduce | flops 1 | bytes 8 | tf_op jit(solution)/shard_map/psum | solution.py:89
  1356.4 9.6 multiply_reduce_fusion.4
  1366.1 22.3 %psum.85 = f32[2048]{0:T(1024)S(1)} all-reduce(f32[2048]{0:T(1024)S(1)} %get-tuple-element.150), channel_id=1, replica_groups=mesh['dp'=64,'mp'=8] {'mp'}, use_global_device_ids=true, to_apply=%region_19.20 | all-reduce | flops 2048 | bytes 16384 | tf_op jit(solution)/shard_map/psum | solution.py:100
  1388.4 7.6 fusion.7
  1395.9 0.0 all-reduce.11.cloned.1.call-update
  1395.9 527.8 %all-reduce.11.cloned.1.call-done = f32[2560,128]{0,1:T(8,128)} async-done(((f32[2560,128]{0,1:T(8,128)}), f32[2560,128]{0,1:T(8,128)}) %all-reduce.11.cloned.1.call-update) | async-done | bytes 1310736 | tf_op jit(solution)/shard_map/psum | solution.py:102
  1923.8 3.2 multiply_reduce_fusion
  1927.6 27.9 %psum.87 = f32[]{:T(128)} all-reduce(f32[]{:T(128)} %multiply_reduce_fusion), channel_id=1, replica_groups=mesh['dp'=64,'mp'=8] {'mp'}, use_global_device_ids=true, to_apply=%region_22.23 | all-reduce | flops 1 | bytes 8 | tf_op jit(solution)/shard_map/psum | solution.py:89
  1957.6 3.2 add_multiply_fusion
  1960.9 2.8 copy.23
  (147 shorter events, 3.8 us)
Async XLA Ops:
  6.5 149.3 %copy-start = (bf16[512,2560]{1,0:T(8,128)(2,1)S(1)}, bf16[512,2560]{1,0:T(8,128)(2,1)}, u32[]{:S(2)}) copy-start(bf16[512,2560]{1,0:T(8,128)(2,1)} %param.12) | copy-start | bytes 7864324
  6.5 728.2 %all-reduce.7.cloned.1.call-start = ((), (), s32[]{:S(2)}) async-start(), calls=%async_computation | async-start | bytes 2621440 | tf_op jit(solution)/shard_map/psum | solution.py:86
  155.9 2.1 copy-start.2
  155.9 2.1 copy-start.3
  158.0 47.7 %copy-start.5 = (s32[512]{0:T(512)S(1)}, s32[512]{0:T(512)}, u32[]{:S(2)}) copy-start(s32[512]{0:T(512)} %param.16) | copy-start | bytes 6148
  158.0 47.8 %copy-start.4 = (f32[512]{0:T(512)S(1)}, f32[512]{0:T(512)}, u32[]{:S(2)}) copy-start(f32[512]{0:T(512)} %param.20) | copy-start | bytes 6148
  207.4 0.7 copy-start.1
  207.4 1092.1 %all-reduce.9.cloned.1.call-start = ((), (), s32[]{:S(2)}) async-start(), calls=%async_computation.1 | async-start | bytes 2621440 | tf_op jit(solution)/shard_map/psum | solution.py:102
  779.0 1144.8 %all-reduce.11.cloned.1.call-start = ((), (), s32[]{:S(2)}) async-start(), calls=%async_computation.2 | async-start | bytes 2621440 | tf_op jit(solution)/shard_map/psum | solution.py:102
Sparse Core Ops, SparseCore 0:
  207.5 527.1 all-reduce.6
  779.1 520.3 all-reduce.8
  1396.1 527.6 all-reduce.10
where the time goes:
time: 1970 us
  waiting for transfers between devices  1550 us (79%)
  blocking collectives  314 us (16%)
  matrix products  38.1 us (2%)
  local copies, waits for them, and re-layouts  30.4 us (2%)
    psum x2, waiting for transfers between devices, per_device(): summed = lax.psum(transpose_product(sampled, weighted), 'dp')  1050 us
    psum x1, waiting for transfers between devices, per_device(): grad = lax.psum(transpose_product(hidden_states, logit_grad), 'dp')  505 us
    psum x1, blocking collectives, per_device(): adv_total = lax.psum(jnp.sum(advantage), 'dp')  140 us
    psum x3, blocking collectives, global_dots(): return lax.psum((terms[0],), 'mp')  76.8 us
    psum x2, blocking collectives, per_device(): centre = lax.psum(jnp.sum(sprobs * fisher_lifted, axis=1), 'mp')  49.7 us
  transfers between devices with their start and end apart: 3, of which 3 were waited for; matrix products, arithmetic and copies ran while one was open for 1% of the time, Pallas kernels for 0%

commit v1 on v0

v1 whole, which is shorter than its diff:
```python
import functools
import math

import jax
import jax.numpy as jnp
from jax import lax
from jax.experimental import pallas as pl
from jax.experimental.pallas import tpu as pltpu
from jax.sharding import PartitionSpec as P

D = 2560
A = 1024
AGENTS = 8
SEQ_LEN = 64
GAMMA = 0.99
TRACE_DECAY = 0.95
DAMPING = 0.001
RADIUS_SHARE = 0.001

MESH = pl.DeviceIdType.MESH
F32 = jnp.float32
BF16 = jnp.bfloat16
NY = 8
NZ = 4
NM = 8
ROWS = 512
SAMPLES = 2048
COLS = 128
QUARTER = D // NZ
FAR_FIRST = (4, 3, 5, 2, 6, 1, 7)
NEAR_FIRST = (1, 7, 2, 6, 3, 5, 4)


def kernel(
    hidden, head, bias, ids, actions, rewards, values, starts, ratio, samples,
    out,
    probs, logit_grad, part, grad, image,
    peak_box, centre_box, final_box, dots_m, dots_y, dots_q, adv_y, adv_q, curv_y, curv_q,
    core_box, sum_box, y_box, z_own, z_box,
    small_s, small_r, rs_core_s, rs_core_r, rs_y_s, rs_y_r, rs_z_s, rs_z_r,
    ag_z_s, ag_z_r, ag_y_s, ag_y_r, ag_c_s, ag_c_r,
):
    dp, me_m = lax.axis_index("dp"), lax.axis_index("mp")
    core = lax.rem(dp, 2)
    y = lax.rem(dp // 2, NY)
    z = dp // (2 * NY)
    q = z * 2 + core

    def at_y(k):
        return ((z * NY + k) * 2 + core, me_m)

    def at_q(k):
        return ((k // 2 * NY + y) * 2 + lax.rem(k, 2), me_m)

    def at_z(k):
        return ((k * NY + y) * 2 + core, me_m)

    def at_m(k):
        return (dp, k)

    other = (dp + 1 - 2 * core, me_m)

    barrier = pltpu.get_barrier_semaphore()
    for o in range(1, 8):
        for target in (
            at_y(lax.rem(y + o, NY)),
            at_q(lax.rem(q + o, 8)),
            at_m(lax.rem(me_m + o, NM)),
        ):
            pl.semaphore_signal(barrier, inc=1, device_id=target, device_id_type=MESH)
    pl.semaphore_wait(barrier, 21)

    def copy(src, dst, send, recv, target):
        return pltpu.make_async_remote_copy(
            src_ref=src, dst_ref=dst, send_sem=send, recv_sem=recv,
            device_id=target, device_id_type=MESH,
        )

    def swap_start(n, box, me, place):
        for o in range(1, 8):
            copy(
                box.at[me], box.at[me], small_s.at[n, o], small_r.at[n, me],
                place(lax.rem(me + o, 8)),
            ).start()

    def swap_wait(n, box, me, place):
        for o in range(1, 8):
            k = lax.rem(me + o, 8)
            c = copy(box.at[k], box.at[k], small_s.at[n, o], small_r.at[n, k], place(k))
            c.wait_send()
            c.wait_recv()

    def total(box):
        acc = box[0]
        for k in range(1, 8):
            acc = acc + box[k]
        return acc

    def lane_part(row):
        return row[:, 0:128] + row[:, 128:256] + row[:, 256:384] + row[:, 384:512]

    def ahead(x, s):
        return pltpu.roll(x, ROWS - s, 1)

    def wide(ref):
        return jnp.broadcast_to(ref[...].astype(F32), (8, ROWS))

    position = lax.broadcasted_iota(jnp.int32, (8, ROWS), 1)
    value = wide(values)
    ends = (lax.rem(position, SEQ_LEN) == SEQ_LEN - 1) | (ahead(wide(starts), 1) > 0.5)
    continues = jnp.where(ends, 0.0, 1.0)
    advantage = wide(rewards) + GAMMA * continues * ahead(value, 1) - value
    keeps = GAMMA * TRACE_DECAY * continues
    for s in (1, 2, 4, 8, 16, 32):
        advantage = advantage + keeps * ahead(advantage, s)
        keeps = keeps * ahead(keeps, s)
    advantage = advantage[0:1]
    adv_y[y] = lane_part(advantage)
    swap_start(0, adv_y, y, at_y)

    logits = jnp.dot(hidden[...], head[...], preferred_element_type=F32).T
    bias_t = bias[...].T
    agent = ids[...]
    for k in range(AGENTS):
        logits = logits + jnp.where(agent == k, bias_t[:, k : k + 1], 0.0)
    peak = jnp.max(logits, axis=0, keepdims=True)
    exponent = jnp.exp(logits - peak)
    peak_box[me_m, 0:1] = peak
    peak_box[me_m, 1:2] = jnp.sum(exponent, axis=0, keepdims=True)
    probs[...] = exponent
    swap_start(1, peak_box, me_m, at_m)

    swap_wait(0, adv_y, y, at_y)
    adv_q[q] = total(adv_y)
    swap_start(2, adv_q, q, at_q)

    local = samples[...] - dp * ROWS
    high = lax.shift_right_logical(local, 7)
    low = lax.bitwise_and(local, 127)
    high_hot = (lax.broadcasted_iota(jnp.int32, (8, SAMPLES), 0) == high).astype(F32).astype(BF16)
    low_hot = (lax.broadcasted_iota(jnp.int32, (128, SAMPLES), 0) == low).astype(F32).astype(BF16)
    tally = lax.dot_general(
        high_hot, low_hot, (((1,), (1,)), ((), ())), preferred_element_type=F32
    )
    count = jnp.concatenate([tally[0:1], tally[1:2], tally[2:3], tally[3:4]], axis=1)

    swap_wait(1, peak_box, me_m, at_m)
    row_peak = peak_box[0, 0:1]
    for k in range(1, NM):
        row_peak = jnp.maximum(row_peak, peak_box[k, 0:1])
    denominator = peak_box[0, 1:2] * jnp.exp(peak_box[0, 0:1] - row_peak)
    for k in range(1, NM):
        denominator = denominator + peak_box[k, 1:2] * jnp.exp(peak_box[k, 0:1] - row_peak)
    prob = probs[...] * (jnp.exp(peak - row_peak) / denominator)
    probs[...] = prob

    swap_wait(2, adv_q, q, at_q)
    tokens = ROWS * 64
    adv_mean = jnp.sum(total(adv_q), axis=1, keepdims=True) / tokens
    weight = ratio[...] * (advantage - adv_mean) / tokens
    picked = lax.broadcasted_iota(jnp.int32, (COLS, ROWS), 0) == actions[...] - me_m * COLS
    logit_grad[...] = (weight * (jnp.where(picked, 1.0, 0.0) - prob)).astype(BF16)

    def project():
        for j in range(5):
            cols = slice(512 * j, 512 * (j + 1))
            part[:, :, cols] = jnp.dot(
                logit_grad[...], hidden[:, cols], preferred_element_type=F32
            ).reshape(16, 8, 512)

    def scatter(n):
        sends = []
        for o in FAR_FIRST + (0,):
            c = copy(
                part.at[(1 - core) * 8 + lax.rem(y + o, NY)], core_box.at[n, o],
                rs_core_s.at[n, o], rs_core_r.at[n, o], other,
            )
            c.start()
            sends.append(c)
        for o in FAR_FIRST + (0,):
            k = lax.rem(y + o, NY)
            copy(
                part.at[core * 8 + k], core_box.at[n, o],
                rs_core_s.at[n, o], rs_core_r.at[n, o], other,
            ).wait_recv()
            sum_box[n, o] = part[core * 8 + k] + core_box[n, o]
            if o:
                c = copy(
                    sum_box.at[n, o], y_box.at[n, o], rs_y_s.at[n, o], rs_y_r.at[n, o], at_y(k)
                )
                c.start()
                sends.append(c)
        acc = sum_box[n, 0]
        for o in NEAR_FIRST:
            copy(
                sum_box.at[n, o], y_box.at[n, o], rs_y_s.at[n, o], rs_y_r.at[n, o],
                at_y(lax.rem(y + NY - o, NY)),
            ).wait_recv()
            acc = acc + y_box[n, o]
        for k in range(NZ):
            z_own[n, k] = acc[:, QUARTER * k : QUARTER * (k + 1)]
        for o in (3, 2, 1):
            k = lax.rem(z + o, NZ)
            c = copy(z_own.at[n, k], z_box.at[n, o], rs_z_s.at[n, o], rs_z_r.at[n, o], at_z(k))
            c.start()
            sends.append(c)
        shard = z_own[n, z]
        for o in (1, 2, 3):
            k = lax.rem(z + NZ - o, NZ)
            copy(
                z_own.at[n, k], z_box.at[n, o], rs_z_s.at[n, o], rs_z_r.at[n, o], at_z(k)
            ).wait_recv()
            shard = shard + z_box[n, o]
        for c in sends:
            c.wait_send()
        return shard

    columns = pl.ds(pl.multiple_of(z * QUARTER, 128), QUARTER)

    def gather_start(n, full):
        mine = core * 8 + y
        sends = []
        piece = full.at[mine, :, columns]
        for o in (3, 2, 1):
            c = copy(
                piece, piece, ag_z_s.at[n, o], ag_z_r.at[n, o], at_z(lax.rem(z + o, NZ))
            )
            c.start()
            sends.append(c)
        for o in (1, 2, 3):
            k = lax.rem(z + NZ - o, NZ)
            there = full.at[mine, :, pl.ds(pl.multiple_of(k * QUARTER, 128), QUARTER)]
            copy(there, there, ag_z_s.at[n, o], ag_z_r.at[n, o], at_z(k)).wait_recv()
        whole = full.at[mine]
        for o in FAR_FIRST:
            c = copy(
                whole, whole, ag_y_s.at[n, o], ag_y_r.at[n, o], at_y(lax.rem(y + o, NY))
            )
            c.start()
            sends.append(c)
        c = copy(whole, whole, ag_c_s.at[n, 0], ag_c_r.at[n, 0], other)
        c.start()
        sends.append(c)
        return sends

    def gather_wait(n, full, sends):
        for o in NEAR_FIRST:
            k = lax.rem(y + NY - o, NY)
            there = full.at[core * 8 + k]
            copy(there, there, ag_y_s.at[n, o], ag_y_r.at[n, o], at_y(k)).wait_recv()
            c = copy(there, there, ag_c_s.at[n, o], ag_c_r.at[n, o], other)
            c.start()
            sends.append(c)
        for o in (0,) + NEAR_FIRST:
            there = full.at[(1 - core) * 8 + lax.rem(y + NY - o, NY)]
            copy(there, there, ag_c_s.at[n, o], ag_c_r.at[n, o], other).wait_recv()
        for c in sends:
            c.wait_send()

    def lift(vector):
        return lax.dot_general(
            vector.reshape(COLS, D).astype(BF16), hidden[...], (((1,), (1,)), ((), ())),
            preferred_element_type=F32,
        )

    project()
    grad_piece = scatter(0)
    grad[core * 8 + y, :, columns] = grad_piece
    gather_wait(0, grad, gather_start(0, grad))

    lifted = lift(grad[...])
    prob = probs[...]
    centre_box[me_m] = jnp.sum(prob * lifted, axis=0, keepdims=True)
    swap_start(3, centre_box, me_m, at_m)
    swap_wait(3, centre_box, me_m, at_m)
    logit_grad[...] = (count * (prob * (lifted - total(centre_box)))).astype(BF16)
    project()
    image_piece = scatter(1) / (SAMPLES * 64) + DAMPING * grad_piece
    image[core * 8 + y, :, columns] = image_piece
    sends = gather_start(1, image)

    def folded(x):
        acc = x[:, 0:128]
        for k in range(1, 5):
            acc = acc + x[:, 128 * k : 128 * (k + 1)]
        return jnp.sum(acc, axis=0, keepdims=True)

    dots_m[me_m, 0:1] = folded(grad_piece * grad_piece)
    dots_m[me_m, 1:2] = folded(grad_piece * image_piece)
    dots_m[me_m, 2:3] = folded(image_piece * image_piece)
    dots_m[me_m, 3:8] = jnp.zeros((5, 128), F32)
    swap_start(4, dots_m, me_m, at_m)
    swap_wait(4, dots_m, me_m, at_m)
    dots_y[y] = total(dots_m)
    swap_start(5, dots_y, y, at_y)
    swap_wait(5, dots_y, y, at_y)
    dots_q[q] = total(dots_y)
    swap_start(6, dots_q, q, at_q)
    swap_wait(6, dots_q, q, at_q)
    dots = jnp.sum(total(dots_q), axis=1, keepdims=True)
    rr, curvature, image_sq = dots[0:1], dots[1:2], dots[2:3]
    step = rr / curvature
    rr_next = rr - 2.0 * step * curvature + step * step * image_sq
    beta = rr_next / rr
    quad = step * step * curvature
    gather_wait(1, image, sends)

    def direction():
        g = grad[...].reshape(COLS, D)
        return g, g - step * image[...].reshape(COLS, D) + beta * g

    lifted = lift(direction()[1])
    prob = probs[...]
    mass = jnp.sum(prob, axis=0, keepdims=True)
    moment = jnp.sum(prob * lifted, axis=0, keepdims=True)
    mean = jnp.where(mass > 0.0, moment / jnp.where(mass > 0.0, mass, 1.0), 0.0)
    spread = lifted - mean
    final_box[me_m, 0:1] = moment
    final_box[me_m, 1:2] = jnp.sum(prob * spread * spread, axis=0, keepdims=True)
    swap_start(7, final_box, me_m, at_m)
    swap_wait(7, final_box, me_m, at_m)
    sums = total(final_box)
    centre, variance = sums[0:1], sums[1:2]
    for k in range(NM):
        mass = peak_box[k, 1:2] * (jnp.exp(peak_box[k, 0:1] - row_peak) / denominator)
        mean = jnp.where(mass > 0.0, final_box[k, 0:1] / jnp.where(mass > 0.0, mass, 1.0), 0.0)
        variance = variance + mass * (mean - centre) * (mean - centre)
    curv_y[y] = lane_part(count * variance)
    swap_start(8, curv_y, y, at_y)
    swap_wait(8, curv_y, y, at_y)
    curv_q[q] = total(curv_y)
    swap_start(9, curv_q, q, at_q)
    swap_wait(9, curv_q, q, at_q)
    curvature = jnp.sum(total(curv_q), axis=1, keepdims=True) / (SAMPLES * 64)
    curvature = curvature + DAMPING * (rr_next + beta * beta * rr)
    last = rr_next / curvature
    quad = quad + last * last * curvature
    scale = jnp.sqrt(D * A * RADIUS_SHARE / quad)
    g, d = direction()
    out[...] = (step * g + last * d) * scale


def per_device(hidden, head, bias, ids, actions, rewards, values, starts, ratio, samples):
    dma = pltpu.SemaphoreType.DMA
    vmem = pltpu.VMEM

    def row(x):
        return x.reshape(1, -1)

    result = pl.pallas_call(
        kernel,
        out_shape=jax.ShapeDtypeStruct((COLS, D), F32),
        in_specs=[pl.BlockSpec(memory_space=pltpu.VMEM)] * 10,
        out_specs=pl.BlockSpec(memory_space=pltpu.VMEM),
        scratch_shapes=[
            vmem((COLS, ROWS), F32),
            vmem((COLS, ROWS), BF16),
            vmem((16, 8, D), F32),
            vmem((16, 8, D), F32),
            vmem((16, 8, D), F32),
            vmem((8, 2, ROWS), F32),
            vmem((8, 1, ROWS), F32),
            vmem((8, 2, ROWS), F32),
            vmem((8, 8, 128), F32),
            vmem((8, 8, 128), F32),
            vmem((8, 8, 128), F32),
            vmem((8, 1, 128), F32),
            vmem((8, 1, 128), F32),
            vmem((8, 1, 128), F32),
            vmem((8, 1, 128), F32),
            vmem((2, 8, 8, D), F32),
            vmem((2, 8, 8, D), F32),
            vmem((2, 8, 8, D), F32),
            vmem((2, NZ, 8, QUARTER), F32),
            vmem((2, NZ, 8, QUARTER), F32),
            dma((10, 8)),
            dma((10, 8)),
            dma((2, 8)),
            dma((2, 8)),
            dma((2, 8)),
            dma((2, 8)),
            dma((2, NZ)),
            dma((2, NZ)),
            dma((2, NZ)),
            dma((2, NZ)),
            dma((2, 8)),
            dma((2, 8)),
            dma((2, 8)),
            dma((2, 8)),
        ],
        compiler_params=pltpu.CompilerParams(
            collective_id=0, has_side_effects=True, vmem_limit_bytes=48 * 1024 * 1024
        ),
        name="step",
    )(
        hidden, head, bias, row(ids), row(actions), row(rewards), row(values), row(starts),
        row(ratio), row(samples),
    )
    return result.T


def solution(mesh):
    placed = (P("dp", None), P(None, "mp"), P(None, "mp")) + (P("dp"),) * 7
    return jax.shard_map(
        per_device, mesh=mesh, in_specs=placed, out_specs=P(None, "mp"), check_vma=False
    )
```

time: 1970 us -> 152 us (0.08)
  waiting for transfers between devices: 1550 us -> 0 us
  blocking collectives: 314 us -> 0 us
  Pallas kernels: 0 us -> 142 us
  matrix products: 38.1 us -> 0 us
  local copies, waits for them, and re-layouts: 30.4 us -> 9.76 us
    psum x3 -> x0, waiting for transfers between devices: 1550 us -> none  [the longest x2 1050 us: per_device(): summed = lax.psum(transpose_product(sampled, weighted), 'dp')]
    psum x7 -> x0, blocking collectives: 287 us -> none  [the longest x1 140 us: per_device(): adv_total = lax.psum(jnp.sum(advantage), 'dp')]
    pallas_call x0 -> x1, Pallas kernels: none -> 142 us  [per_device(): pl.pallas_call(kernel, out_shape=jax.ShapeDtypeStruct((COLS, D), F32), in...]
    dot_general x7 -> x0, matrix products: 38.1 us -> none  [the longest x2 18.9 us: per_device(): jnp.dot(sampled, direction.astype(jnp.bfloat16), preferred_element_type=j...]
    pmax x1 -> x0, blocking collectives: 26.7 us -> none  [per_device(): row_peak = lax.pmax(local_peak, 'mp')]
    gather x3 -> x0, local copies, waits for them, and re-layouts: 21.6 us -> none  [the longest x1 11.5 us: per_device(): sampled = jnp.take(hidden_states, local_rows, axis=0)]
  transfers between devices with their start and end apart: 3 -> 0, of which waited for: 3 -> 0; matrix products, arithmetic and copies ran while one was open for 1% -> 0% of each run, Pallas kernels for 0% -> 0%
where the time goes in v1:
time: 152 us; the launch traced here: 151 us
  Pallas kernels  142 us (93%)
  local copies, waits for them, and re-layouts  9.76 us (6%)
    pallas_call x1, Pallas kernels, per_device(): pl.pallas_call(kernel, out_shape=jax.ShapeDtypeStruct((COLS, D), F32), in...  142 us
    unnamed x20, local copies, waits for them, and re-layouts  8.3 us

profile of v1, /device:TPU:1, one launch (start us, length us, event | category | flops | bytes accessed | tf_op | source)
XLA Modules:
  0.0 151.4 jit_solution(1055169504286506418)
XLA Ops:
  0.0 0.0 copy-start
  0.0 1.7 %copy-done = bf16[512,2560]{1,0:T(8,128)(2,1)S(1)} copy-done((bf16[512,2560]{1,0:T(8,128)(2,1)S(1)}, bf16[512,2560]{1,0:T(8,128)(2,1)}, u32[]{:S(2)}) %copy-start) | copy-done | bytes 2621464
  1.7 0.0 copy-start.1
  1.7 1.1 copy-done.1
  2.8 0.0 copy-start.2
  2.8 0.7 copy-done.2
  3.5 0.0 copy-start.3
  3.5 0.7 copy-done.3
  4.2 0.0 copy-start.4
  4.2 0.7 copy-done.4
  4.9 0.0 copy-start.5
  4.9 0.7 copy-done.5
  5.6 0.0 copy-start.6
  5.6 0.7 copy-done.6
  6.3 0.0 copy-start.7
  6.3 0.7 copy-done.7
  6.9 0.0 copy-start.8
  6.9 0.7 copy-done.8
  7.6 0.0 copy-start.9
  7.6 0.7 copy-done.9
  8.3 141.6 %step.1 = f32[128,2560]{1,0:T(8,128)S(1)} custom-call(bf16[512,2560]{1,0:T(8,128)(2,1)S(1)} %copy-done, bf16[2560,128]{1,0:T(8,128)(2,1)S(1)} %copy-done.1, f32[8,128]{1,0:T(8,128)S(1)} %copy-done.3, s32[1,512]{1,0:T(1,128)S(1)} %bitcast.10, s32[1,512]{1,0:T(1,128)S(1)} %bitcast.11, f32[1,512]{1,0:T(1,128)S(1)} %bitcast.12, f32[1,512]{1,0:T(1,128)S(1)} %bitcast.13, ...), custom_call_target="tpu_custom_call" | custom-call | tf_op jit(solution)/shard_map/step/pallas_call | solution.py:350
  149.9 1.5 copy.11
Async XLA Ops:
  0.0 1.7 %copy-start = (bf16[512,2560]{1,0:T(8,128)(2,1)S(1)}, bf16[512,2560]{1,0:T(8,128)(2,1)}, u32[]{:S(2)}) copy-start(bf16[512,2560]{1,0:T(8,128)(2,1)} %hidden.1) | copy-start | bytes 7864324
  1.7 1.1 copy-start.1
  2.8 0.7 copy-start.2
  3.5 0.7 copy-start.3
  4.2 0.7 copy-start.4
  4.9 0.7 copy-start.5
  5.6 0.7 copy-start.6
  6.3 0.7 copy-start.7
  6.9 0.7 copy-start.8
  7.6 0.7 copy-start.9

commit v2 on v1

--- a/solution.py
+++ b/solution.py
@@ -26,20 +26,38 @@
 ROWS = 512
 SAMPLES = 2048
 COLS = 128
-QUARTER = D // NZ
+LEFT = 1536
 FAR_FIRST = (4, 3, 5, 2, 6, 1, 7)
 NEAR_FIRST = (1, 7, 2, 6, 3, 5, 4)
+CORE_ORDER = (
+    ("a", 4), ("b", 3), ("a", 3), ("a", 5), ("b", 1), ("a", 2), ("a", 6), ("b", 2),
+    ("a", 1), ("a", 7), ("a", 0), ("b", 0),
+)
 
 
 def kernel(
-    hidden, head, bias, ids, actions, rewards, values, starts, ratio, samples,
+    hidden_in, head_in, bias_in, ids_in, actions_in, rewards_in, values_in, starts_in, ratio_in, samples_in,
     out,
-    probs, logit_grad, part, grad, image,
+    hidden, head, bias, ids, actions, rewards, values, starts, ratio, samples, loads,
+    probs, logit_grad, part, grad_hi, grad_lo, image_hi,
     peak_box, centre_box, final_box, dots_m, dots_y, dots_q, adv_y, adv_q, curv_y, curv_q,
-    core_box, sum_box, y_box, z_own, z_box,
-    small_s, small_r, rs_core_s, rs_core_r, rs_y_s, rs_y_r, rs_z_s, rs_z_r,
-    ag_z_s, ag_z_r, ag_y_s, ag_y_r, ag_c_s, ag_c_r,
+    core_a, core_b, send_a32, send_b32, y_a32, z_b32, send_a16, send_b16, y_a16, z_b16,
+    own_a, own_b, z_a, y_b,
+    small_s, small_r, rs_s, rs_r, ag_s, ag_r,
 ):
+    fetches = [
+        pltpu.make_async_copy(src, dst, loads.at[k])
+        for k, (src, dst) in enumerate(
+            (
+                (rewards_in, rewards), (values_in, values), (starts_in, starts),
+                (hidden_in, hidden), (head_in, head), (bias_in, bias), (ids_in, ids),
+                (actions_in, actions), (ratio_in, ratio), (samples_in, samples),
+            )
+        )
+    ]
+    for fetch in fetches:
+        fetch.start()
+
     dp, me_m = lax.axis_index("dp"), lax.axis_index("mp")
     core = lax.rem(dp, 2)
     y = lax.rem(dp // 2, NY)
@@ -98,6 +116,9 @@
 
     def lane_part(row):
         return row[:, 0:128] + row[:, 128:256] + row[:, 256:384] + row[:, 384:512]
+
+    for fetch in fetches[:3]:
+        fetch.wait()
 
     def ahead(x, s):
         return pltpu.roll(x, ROWS - s, 1)
@@ -118,6 +139,9 @@
     adv_y[y] = lane_part(advantage)
     swap_start(0, adv_y, y, at_y)
 
+    for fetch in fetches[3:]:
+        fetch.wait()
+
     logits = jnp.dot(hidden[...], head[...], preferred_element_type=F32).T
     bias_t = bias[...].T
     agent = ids[...]
@@ -168,94 +192,156 @@
                 logit_grad[...], hidden[:, cols], preferred_element_type=F32
             ).reshape(16, 8, 512)
 
-    def scatter(n):
+    def scatter(n, send_a, send_b, y_a, z_b):
+        def core_copy(kind, o):
+            if kind == "a":
+                k = (1 - core) * 8 + lax.rem(y + o, NY)
+                return copy(
+                    part.at[k, :, 0:LEFT], core_a.at[n, o], rs_s.at[n, 0, o], rs_r.at[n, 0, o], other
+                )
+            k = (1 - core) * 8 + lax.rem(z + o, NZ) * 2
+            return copy(
+                part.at[pl.ds(k, 2), :, LEFT:D], core_b.at[n, o],
+                rs_s.at[n, 1, o], rs_r.at[n, 1, o], other,
+            )
+
+        def leg_a(o, k):
+            return copy(send_a.at[o], y_a.at[o], rs_s.at[n, 2, o], rs_r.at[n, 2, o], at_y(k))
+
+        def leg_b(o, k):
+            return copy(send_b.at[o], z_b.at[o], rs_s.at[n, 3, o], rs_r.at[n, 3, o], at_z(k))
+
         sends = []
-        for o in FAR_FIRST + (0,):
-            c = copy(
-                part.at[(1 - core) * 8 + lax.rem(y + o, NY)], core_box.at[n, o],
-                rs_core_s.at[n, o], rs_core_r.at[n, o], other,
-            )
+        for kind, o in CORE_ORDER:
+            c = core_copy(kind, o)
             c.start()
             sends.append(c)
-        for o in FAR_FIRST + (0,):
+        for kind, o in CORE_ORDER:
+            core_copy(kind, o).wait_recv()
+            if kind == "a":
+                k = lax.rem(y + o, NY)
+                term = part[core * 8 + k, :, 0:LEFT] + core_a[n, o]
+                if o == 0:
+                    acc_a = term
+                    continue
+                send_a[o] = term.astype(send_a.dtype)
+                c = leg_a(o, k)
+            else:
+                k = lax.rem(z + o, NZ)
+                term = part[pl.ds(core * 8 + 2 * k, 2), :, LEFT:D] + core_b[n, o]
+                if o == 0:
+                    acc_b = term
+                    continue
+                send_b[o] = term.astype(send_b.dtype)
+                c = leg_b(o, k)
+            c.start()
+            sends.append(c)
+        for o in (1, 2, 3):
+            leg_b(o, lax.rem(z + NZ - o, NZ)).wait_recv()
+            acc_b = acc_b + z_b[o].astype(F32)
+        for k in range(NY):
+            own_b[n, k] = acc_b[k // 4, :, 256 * (k % 4) : 256 * (k % 4 + 1)]
+        for o in FAR_FIRST:
             k = lax.rem(y + o, NY)
-            copy(
-                part.at[core * 8 + k], core_box.at[n, o],
-                rs_core_s.at[n, o], rs_core_r.at[n, o], other,
-            ).wait_recv()
-            sum_box[n, o] = part[core * 8 + k] + core_box[n, o]
-            if o:
-                c = copy(
-                    sum_box.at[n, o], y_box.at[n, o], rs_y_s.at[n, o], rs_y_r.at[n, o], at_y(k)
-                )
-                c.start()
-                sends.append(c)
-        acc = sum_box[n, 0]
+            c = copy(own_b.at[n, k], y_b.at[n, o], rs_s.at[n, 4, o], rs_r.at[n, 4, o], at_y(k))
+            c.start()
+            sends.append(c)
         for o in NEAR_FIRST:
-            copy(
-                sum_box.at[n, o], y_box.at[n, o], rs_y_s.at[n, o], rs_y_r.at[n, o],
-                at_y(lax.rem(y + NY - o, NY)),
-            ).wait_recv()
-            acc = acc + y_box[n, o]
+            leg_a(o, lax.rem(y + NY - o, NY)).wait_recv()
+            acc_a = acc_a + y_a[o].astype(F32)
         for k in range(NZ):
-            z_own[n, k] = acc[:, QUARTER * k : QUARTER * (k + 1)]
+            own_a[n, k] = acc_a[:, 384 * k : 384 * (k + 1)]
         for o in (3, 2, 1):
             k = lax.rem(z + o, NZ)
-            c = copy(z_own.at[n, k], z_box.at[n, o], rs_z_s.at[n, o], rs_z_r.at[n, o], at_z(k))
+            c = copy(own_a.at[n, k], z_a.at[n, o], rs_s.at[n, 5, o], rs_r.at[n, 5, o], at_z(k))
             c.start()
             sends.append(c)
-        shard = z_own[n, z]
+        shard_b = own_b[n, y]
+        for o in NEAR_FIRST:
+            k = lax.rem(y + NY - o, NY)
+            copy(
+                own_b.at[n, k], y_b.at[n, o], rs_s.at[n, 4, o], rs_r.at[n, 4, o], at_y(k)
+            ).wait_recv()
+            shard_b = shard_b + y_b[n, o]
+        shard_a = own_a[n, z]
         for o in (1, 2, 3):
             k = lax.rem(z + NZ - o, NZ)
             copy(
-                z_own.at[n, k], z_box.at[n, o], rs_z_s.at[n, o], rs_z_r.at[n, o], at_z(k)
+                own_a.at[n, k], z_a.at[n, o], rs_s.at[n, 5, o], rs_r.at[n, 5, o], at_z(k)
             ).wait_recv()
-            shard = shard + z_box[n, o]
+            shard_a = shard_a + z_a[n, o]
         for c in sends:
             c.wait_send()
-        return shard
-
-    columns = pl.ds(pl.multiple_of(z * QUARTER, 128), QUARTER)
+        return shard_a, shard_b
+
+    def spot_a(full, ky, kz):
+        return full.at[core * 8 + ky, :, pl.ds(pl.multiple_of(kz * 384, 128), 384)]
+
+    def spot_b(full, ky, kz):
+        columns = pl.ds(pl.multiple_of(LEFT + lax.rem(ky, 4) * 256, 128), 256)
+        return full.at[core * 8 + 2 * kz + ky // 4, :, columns]
+
+    def line_a(full, kc, ky):
+        return full.at[kc * 8 + ky, :, 0:LEFT]
+
+    def line_b(full, kc, kz):
+        return full.at[pl.ds(kc * 8 + 2 * kz, 2), :, LEFT:D]
 
     def gather_start(n, full):
-        mine = core * 8 + y
         sends = []
-        piece = full.at[mine, :, columns]
-        for o in (3, 2, 1):
-            c = copy(
-                piece, piece, ag_z_s.at[n, o], ag_z_r.at[n, o], at_z(lax.rem(z + o, NZ))
-            )
+
+        def begin(ref, kind, o, target):
+            c = copy(ref, ref, ag_s.at[n, kind, o], ag_r.at[n, kind, o], target)
             c.start()
             sends.append(c)
+
+        for o in (3, 2, 1):
+            begin(spot_a(full, y, z), 0, o, at_z(lax.rem(z + o, NZ)))
+        for o in FAR_FIRST:
+            begin(spot_b(full, y, z), 1, o, at_y(lax.rem(y + o, NY)))
         for o in (1, 2, 3):
             k = lax.rem(z + NZ - o, NZ)
-            there = full.at[mine, :, pl.ds(pl.multiple_of(k * QUARTER, 128), QUARTER)]
-            copy(there, there, ag_z_s.at[n, o], ag_z_r.at[n, o], at_z(k)).wait_recv()
-        whole = full.at[mine]
+            there = spot_a(full, y, k)
+            copy(there, there, ag_s.at[n, 0, o], ag_r.at[n, 0, o], at_z(k)).wait_recv()
         for o in FAR_FIRST:
-            c = copy(
-                whole, whole, ag_y_s.at[n, o], ag_y_r.at[n, o], at_y(lax.rem(y + o, NY))
-            )
-            c.start()
-            sends.append(c)
-        c = copy(whole, whole, ag_c_s.at[n, 0], ag_c_r.at[n, 0], other)
-        c.start()
-        sends.append(c)
-        return sends
-
-    def gather_wait(n, full, sends):
+            begin(line_a(full, core, y), 2, o, at_y(lax.rem(y + o, NY)))
+        begin(line_a(full, core, y), 4, 0, other)
         for o in NEAR_FIRST:
             k = lax.rem(y + NY - o, NY)
-            there = full.at[core * 8 + k]
-            copy(there, there, ag_y_s.at[n, o], ag_y_r.at[n, o], at_y(k)).wait_recv()
-            c = copy(there, there, ag_c_s.at[n, o], ag_c_r.at[n, o], other)
-            c.start()
-            sends.append(c)
-        for o in (0,) + NEAR_FIRST:
-            there = full.at[(1 - core) * 8 + lax.rem(y + NY - o, NY)]
-            copy(there, there, ag_c_s.at[n, o], ag_c_r.at[n, o], other).wait_recv()
+            there = spot_b(full, k, z)
+            copy(there, there, ag_s.at[n, 1, o], ag_r.at[n, 1, o], at_y(k)).wait_recv()
+        for o in (3, 2, 1):
+            begin(line_b(full, core, z), 3, o, at_z(lax.rem(z + o, NZ)))
+        begin(line_b(full, core, z), 5, 0, other)
+        return sends
+
+    def gather_wait(n, full, sends):
+        def arrive(ref, kind, o, source, onward):
+            copy(ref, ref, ag_s.at[n, kind, o], ag_r.at[n, kind, o], source).wait_recv()
+            if onward:
+                c = copy(ref, ref, ag_s.at[n, onward, o], ag_r.at[n, onward, o], other)
+                c.start()
+                sends.append(c)
+
+        for kind, o in (("a", 1), ("a", 7), ("b", 1), ("a", 2), ("a", 6), ("b", 2), ("b", 3), ("a", 3), ("a", 5), ("a", 4)):
+            if kind == "a":
+                k = lax.rem(y + NY - o, NY)
+                arrive(line_a(full, core, k), 2, o, at_y(k), 4)
+            else:
+                k = lax.rem(z + NZ - o, NZ)
+                arrive(line_b(full, core, k), 3, o, at_z(k), 5)
+        for o in range(NY):
+            arrive(line_a(full, 1 - core, lax.rem(y + NY - o, NY)), 4, o, other, 0)
+        for o in range(NZ):
+            arrive(line_b(full, 1 - core, lax.rem(z + NZ - o, NZ)), 5, o, other, 0)
         for c in sends:
             c.wait_send()
+
+    def keep(full, shards):
+        shard_a, shard_b = shards
+        full[core * 8 + y, :, pl.ds(pl.multiple_of(z * 384, 128), 384)] = shard_a.astype(BF16)
+        columns = pl.ds(pl.multiple_of(LEFT + lax.rem(y, 4) * 256, 128), 256)
+        full[core * 8 + 2 * z + y // 4, :, columns] = shard_b.astype(BF16)
 
     def lift(vector):
         return lax.dot_general(
@@ -264,30 +350,34 @@
         )
 
     project()
-    grad_piece = scatter(0)
-    grad[core * 8 + y, :, columns] = grad_piece
-    gather_wait(0, grad, gather_start(0, grad))
-
-    lifted = lift(grad[...])
+    grad_piece = scatter(0, send_a32, send_b32, y_a32, z_b32)
+    keep(grad_hi, grad_piece)
+    keep(grad_lo, [x - x.astype(BF16).astype(F32) for x in grad_piece])
+    gather_wait(0, grad_hi, gather_start(0, grad_hi))
+
+    lifted = lift(grad_hi[...].astype(F32))
     prob = probs[...]
     centre_box[me_m] = jnp.sum(prob * lifted, axis=0, keepdims=True)
     swap_start(3, centre_box, me_m, at_m)
     swap_wait(3, centre_box, me_m, at_m)
     logit_grad[...] = (count * (prob * (lifted - total(centre_box)))).astype(BF16)
     project()
-    image_piece = scatter(1) / (SAMPLES * 64) + DAMPING * grad_piece
-    image[core * 8 + y, :, columns] = image_piece
-    sends = gather_start(1, image)
-
-    def folded(x):
-        acc = x[:, 0:128]
-        for k in range(1, 5):
-            acc = acc + x[:, 128 * k : 128 * (k + 1)]
-        return jnp.sum(acc, axis=0, keepdims=True)
-
-    dots_m[me_m, 0:1] = folded(grad_piece * grad_piece)
-    dots_m[me_m, 1:2] = folded(grad_piece * image_piece)
-    dots_m[me_m, 2:3] = folded(image_piece * image_piece)
+    fisher = [x / (SAMPLES * 64) for x in scatter(1, send_a16, send_b16, y_a16, z_b16)]
+    keep(image_hi, fisher)
+    image_piece = [f + DAMPING * g for f, g in zip(fisher, grad_piece)]
+    sends = gather_start(1, image_hi)
+
+    def folded(left, right):
+        terms = [
+            l[:, k : k + 128] * r[:, k : k + 128]
+            for l, r in zip(left, right)
+            for k in range(0, l.shape[1], 128)
+        ]
+        return jnp.sum(sum(terms[1:], terms[0]), axis=0, keepdims=True)
+
+    dots_m[me_m, 0:1] = folded(grad_piece, grad_piece)
+    dots_m[me_m, 1:2] = folded(grad_piece, image_piece)
+    dots_m[me_m, 2:3] = folded(image_piece, image_piece)
     dots_m[me_m, 3:8] = jnp.zeros((5, 128), F32)
     swap_start(4, dots_m, me_m, at_m)
     swap_wait(4, dots_m, me_m, at_m)
@@ -303,13 +393,12 @@
     rr_next = rr - 2.0 * step * curvature + step * step * image_sq
     beta = rr_next / rr
     quad = step * step * curvature
-    gather_wait(1, image, sends)
-
-    def direction():
-        g = grad[...].reshape(COLS, D)
-        return g, g - step * image[...].reshape(COLS, D) + beta * g
-
-    lifted = lift(direction()[1])
+    gather_wait(1, image_hi, sends)
+
+    def direction(g):
+        return g - step * (image_hi[...].astype(F32) + DAMPING * g) + beta * g
+
+    lifted = lift(direction(grad_hi[...].astype(F32)))
     prob = probs[...]
     mass = jnp.sum(prob, axis=0, keepdims=True)
     moment = jnp.sum(prob * lifted, axis=0, keepdims=True)
@@ -318,6 +407,7 @@
     final_box[me_m, 0:1] = moment
     final_box[me_m, 1:2] = jnp.sum(prob * spread * spread, axis=0, keepdims=True)
     swap_start(7, final_box, me_m, at_m)
+    sends = gather_start(2, grad_lo)
     swap_wait(7, final_box, me_m, at_m)
     sums = total(final_box)
     centre, variance = sums[0:1], sums[1:2]
@@ -330,14 +420,15 @@
     swap_wait(8, curv_y, y, at_y)
     curv_q[q] = total(curv_y)
     swap_start(9, curv_q, q, at_q)
+    gather_wait(2, grad_lo, sends)
     swap_wait(9, curv_q, q, at_q)
     curvature = jnp.sum(total(curv_q), axis=1, keepdims=True) / (SAMPLES * 64)
     curvature = curvature + DAMPING * (rr_next + beta * beta * rr)
     last = rr_next / curvature
     quad = quad + last * last * curvature
     scale = jnp.sqrt(D * A * RADIUS_SHARE / quad)
-    g, d = direction()
-    out[...] = (step * g + last * d) * scale
+    g = grad_hi[...].astype(F32) + grad_lo[...].astype(F32)
+    out[...] = ((step * g + last * direction(g)) * scale).reshape(COLS, D)
 
 
 def per_device(hidden, head, bias, ids, actions, rewards, values, starts, ratio, samples):
@@ -350,14 +441,26 @@
     result = pl.pallas_call(
         kernel,
         out_shape=jax.ShapeDtypeStruct((COLS, D), F32),
-        in_specs=[pl.BlockSpec(memory_space=pltpu.VMEM)] * 10,
+        in_specs=[pl.BlockSpec(memory_space=pltpu.MemorySpace.HBM)] * 10,
         out_specs=pl.BlockSpec(memory_space=pltpu.VMEM),
         scratch_shapes=[
+            vmem((ROWS, D), BF16),
+            vmem((D, COLS), BF16),
+            vmem((AGENTS, COLS), F32),
+            vmem((1, ROWS), jnp.int32),
+            vmem((1, ROWS), jnp.int32),
+            vmem((1, ROWS), F32),
+            vmem((1, ROWS), F32),
+            vmem((1, ROWS), jnp.int32),
+            vmem((1, ROWS), F32),
+            vmem((1, SAMPLES), jnp.int32),
+            dma((10,)),
             vmem((COLS, ROWS), F32),
             vmem((COLS, ROWS), BF16),
             vmem((16, 8, D), F32),
-            vmem((16, 8, D), F32),
-            vmem((16, 8, D), F32),
+            vmem((16, 8, D), BF16),
+            vmem((16, 8, D), BF16),
+            vmem((16, 8, D), BF16),
             vmem((8, 2, ROWS), F32),
             vmem((8, 1, ROWS), F32),
             vmem((8, 2, ROWS), F32),
@@ -368,28 +471,29 @@
             vmem((8, 1, 128), F32),
             vmem((8, 1, 128), F32),
             vmem((8, 1, 128), F32),
-            vmem((2, 8, 8, D), F32),
-            vmem((2, 8, 8, D), F32),
-            vmem((2, 8, 8, D), F32),
-            vmem((2, NZ, 8, QUARTER), F32),
-            vmem((2, NZ, 8, QUARTER), F32),
+            vmem((2, NY, 8, LEFT), F32),
+            vmem((2, NZ, 2, 8, D - LEFT), F32),
+            vmem((NY, 8, LEFT), F32),
+            vmem((NZ, 2, 8, D - LEFT), F32),
+            vmem((NY, 8, LEFT), F32),
+            vmem((NZ, 2, 8, D - LEFT), F32),
+            vmem((NY, 8, LEFT), BF16),
+            vmem((NZ, 2, 8, D - LEFT), BF16),
+            vmem((NY, 8, LEFT), BF16),
+            vmem((NZ, 2, 8, D - LEFT), BF16),
+            vmem((2, NZ, 8, 384), F32),
+            vmem((2, NY, 8, 256), F32),
+            vmem((2, NZ, 8, 384), F32),
+            vmem((2, NY, 8, 256), F32),
             dma((10, 8)),
             dma((10, 8)),
-            dma((2, 8)),
-            dma((2, 8)),
-            dma((2, 8)),
-            dma((2, 8)),
-            dma((2, NZ)),
-            dma((2, NZ)),
-            dma((2, NZ)),
-            dma((2, NZ)),
-            dma((2, 8)),
-            dma((2, 8)),
-            dma((2, 8)),
-            dma((2, 8)),
+            dma((2, 6, 8)),
+            dma((2, 6, 8)),
+            dma((3, 6, 8)),
+            dma((3, 6, 8)),
         ],
         compiler_params=pltpu.CompilerParams(
-            collective_id=0, has_side_effects=True, vmem_limit_bytes=48 * 1024 * 1024
+            collective_id=0, has_side_effects=True, vmem_limit_bytes=61 * 1024 * 1024
         ),
         name="step",
     )(

time: 152 us -> 120 us (0.79)
  Pallas kernels: 142 us -> 117 us
  local copies, waits for them, and re-layouts: 9.76 us -> 2.78 us
    pallas_call x1, Pallas kernels: 142 us -> 117 us  [per_device(): pl.pallas_call(kernel, out_shape=jax.ShapeDtypeStruct((COLS, D), F32), in...]
    unnamed x20 -> x0, local copies, waits for them, and re-layouts: 8.3 us -> none
where the time goes in v2:
time: 120 us
  Pallas kernels  117 us (98%)
  local copies, waits for them, and re-layouts  2.78 us (2%)
    pallas_call x1, Pallas kernels, per_device(): pl.pallas_call(kernel, out_shape=jax.ShapeDtypeStruct((COLS, D), F32), in...  117 us
    transpose x1, local copies, waits for them, and re-layouts, per_device(): return result.T  2.78 us

profile of v2, /device:TPU:1, one launch (start us, length us, event | category | flops | bytes accessed | tf_op | source)
XLA Modules:
  0.0 120.1 jit_solution(13293488297565448888)
XLA Ops:
  0.0 117.3 %step.1 = f32[128,2560]{1,0:T(8,128)} custom-call(bf16[512,2560]{1,0:T(8,128)(2,1)} %hidden_in.1, bf16[2560,128]{1,0:T(8,128)(2,1)} %head_in.1, f32[8,128]{1,0:T(8,128)} %bias_in.1, s32[1,512]{1,0:T(1,128)} %bitcast.10, s32[1,512]{1,0:T(1,128)} %bitcast.11, f32[1,512]{1,0:T(1,128)} %bitcast.12, f32[1,512]{1,0:T(1,128)} %bitcast.13, s32[1,512]{1,0:T(1,128)} %bitcast.14, ...), custom_call_target="tpu_custom_call" | custom-call | tf_op jit(solution)/shard_map/step/pallas_call | solution.py:441
  117.4 2.8 %copy.11 = f32[2560,128]{1,0:T(8,128)} copy(f32[2560,128]{0,1:T(8,128)} %bitcast.8) | data formatting | bytes 2621440 | tf_op jit(solution)/shard_map/transpose | solution.py:503

commit v3 on v2

--- a/solution.py
+++ b/solution.py
@@ -45,6 +45,35 @@
     own_a, own_b, z_a, y_b,
     small_s, small_r, rs_s, rs_r, ag_s, ag_r,
 ):
+    dp, me_m = lax.axis_index("dp"), lax.axis_index("mp")
+    core = lax.rem(dp, 2)
+    y = lax.rem(dp // 2, NY)
+    z = dp // (2 * NY)
+    q = z * 2 + core
+
+    def at_y(k):
+        return ((z * NY + k) * 2 + core, me_m)
+
+    def at_q(k):
+        return ((k // 2 * NY + y) * 2 + lax.rem(k, 2), me_m)
+
+    def at_z(k):
+        return ((k * NY + y) * 2 + core, me_m)
+
+    def at_m(k):
+        return (dp, k)
+
+    other = (dp + 1 - 2 * core, me_m)
+
+    barrier = pltpu.get_barrier_semaphore()
+    for o in range(1, 8):
+        for target in (
+            at_y(lax.rem(y + o, NY)),
+            at_q(lax.rem(q + o, 8)),
+            at_m(lax.rem(me_m + o, NM)),
+        ):
+            pl.semaphore_signal(barrier, inc=1, device_id=target, device_id_type=MESH)
+
     fetches = [
         pltpu.make_async_copy(src, dst, loads.at[k])
         for k, (src, dst) in enumerate(
@@ -58,36 +87,6 @@
     for fetch in fetches:
         fetch.start()
 
-    dp, me_m = lax.axis_index("dp"), lax.axis_index("mp")
-    core = lax.rem(dp, 2)
-    y = lax.rem(dp // 2, NY)
-    z = dp // (2 * NY)
-    q = z * 2 + core
-
-    def at_y(k):
-        return ((z * NY + k) * 2 + core, me_m)
-
-    def at_q(k):
-        return ((k // 2 * NY + y) * 2 + lax.rem(k, 2), me_m)
-
-    def at_z(k):
-        return ((k * NY + y) * 2 + core, me_m)
-
-    def at_m(k):
-        return (dp, k)
-
-    other = (dp + 1 - 2 * core, me_m)
-
-    barrier = pltpu.get_barrier_semaphore()
-    for o in range(1, 8):
-        for target in (
-            at_y(lax.rem(y + o, NY)),
-            at_q(lax.rem(q + o, 8)),
-            at_m(lax.rem(me_m + o, NM)),
-        ):
-            pl.semaphore_signal(barrier, inc=1, device_id=target, device_id_type=MESH)
-    pl.semaphore_wait(barrier, 21)
-
     def copy(src, dst, send, recv, target):
         return pltpu.make_async_remote_copy(
             src_ref=src, dst_ref=dst, send_sem=send, recv_sem=recv,
@@ -137,7 +136,6 @@
         keeps = keeps * ahead(keeps, s)
     advantage = advantage[0:1]
     adv_y[y] = lane_part(advantage)
-    swap_start(0, adv_y, y, at_y)
 
     for fetch in fetches[3:]:
         fetch.wait()
@@ -152,11 +150,9 @@
     peak_box[me_m, 0:1] = peak
     peak_box[me_m, 1:2] = jnp.sum(exponent, axis=0, keepdims=True)
     probs[...] = exponent
+    pl.semaphore_wait(barrier, 21)
+    swap_start(0, adv_y, y, at_y)
     swap_start(1, peak_box, me_m, at_m)
-
-    swap_wait(0, adv_y, y, at_y)
-    adv_q[q] = total(adv_y)
-    swap_start(2, adv_q, q, at_q)
 
     local = samples[...] - dp * ROWS
     high = lax.shift_right_logical(local, 7)
@@ -167,6 +163,10 @@
         high_hot, low_hot, (((1,), (1,)), ((), ())), preferred_element_type=F32
     )
     count = jnp.concatenate([tally[0:1], tally[1:2], tally[2:3], tally[3:4]], axis=1)
+
+    swap_wait(0, adv_y, y, at_y)
+    adv_q[q] = total(adv_y)
+    swap_start(2, adv_q, q, at_q)
 
     swap_wait(1, peak_box, me_m, at_m)
     row_peak = peak_box[0, 0:1]
@@ -365,8 +365,6 @@
     fisher = [x / (SAMPLES * 64) for x in scatter(1, send_a16, send_b16, y_a16, z_b16)]
     keep(image_hi, fisher)
     image_piece = [f + DAMPING * g for f, g in zip(fisher, grad_piece)]
-    sends = gather_start(1, image_hi)
-
     def folded(left, right):
         terms = [
             l[:, k : k + 128] * r[:, k : k + 128]
@@ -380,12 +378,14 @@
     dots_m[me_m, 2:3] = folded(image_piece, image_piece)
     dots_m[me_m, 3:8] = jnp.zeros((5, 128), F32)
     swap_start(4, dots_m, me_m, at_m)
+    sends = gather_start(1, image_hi)
     swap_wait(4, dots_m, me_m, at_m)
     dots_y[y] = total(dots_m)
     swap_start(5, dots_y, y, at_y)
     swap_wait(5, dots_y, y, at_y)
     dots_q[q] = total(dots_y)
     swap_start(6, dots_q, q, at_q)
+    gather_wait(1, image_hi, sends)
     swap_wait(6, dots_q, q, at_q)
     dots = jnp.sum(total(dots_q), axis=1, keepdims=True)
     rr, curvature, image_sq = dots[0:1], dots[1:2], dots[2:3]
@@ -393,7 +393,6 @@
     rr_next = rr - 2.0 * step * curvature + step * step * image_sq
     beta = rr_next / rr
     quad = step * step * curvature
-    gather_wait(1, image_hi, sends)
 
     def direction(g):
         return g - step * (image_hi[...].astype(F32) + DAMPING * g) + beta * g
@@ -493,12 +492,17 @@
             dma((3, 6, 8)),
         ],
         compiler_params=pltpu.CompilerParams(
-            collective_id=0, has_side_effects=True, vmem_limit_bytes=61 * 1024 * 1024
+            collective_id=0, has_side_effects=True, vmem_limit_bytes=40 * 1024 * 1024
         ),
         name="step",
     )(
-        hidden, head, bias, row(ids), row(actions), row(rewards), row(values), row(starts),
-        row(ratio), row(samples),
+        *(
+            pltpu.with_memory_space_constraint(x, pltpu.MemorySpace.HBM)
+            for x in (
+                hidden, head, bias, row(ids), row(actions), row(rewards), row(values), row(starts),
+                row(ratio), row(samples),
+            )
+        )
     )
     return result.T
 

time: 120 us -> 109 us (0.908)
  Pallas kernels: 117 us -> 108 us
  local copies, waits for them, and re-layouts: 2.78 us -> 1.46 us
    pallas_call x1, Pallas kernels: 117 us -> 108 us  [per_device(): pl.pallas_call(kernel, out_shape=jax.ShapeDtypeStruct((COLS, D), F32), in...]
    transpose x1, local copies, waits for them, and re-layouts: 2.78 us -> 1.46 us  [per_device(): return result.T]
where the time goes in v3:
time: 109 us
  Pallas kernels  108 us (99%)
  local copies, waits for them, and re-layouts  1.46 us (1%)
    pallas_call x1, Pallas kernels, per_device(): pl.pallas_call(kernel, out_shape=jax.ShapeDtypeStruct((COLS, D), F32), in...  108 us

profile of v3, /device:TPU:1, one launch (start us, length us, event | category | flops | bytes accessed | tf_op | source)
XLA Modules:
  0.0 109.0 jit_solution(3442631895357239922)
XLA Ops:
  0.0 107.6 %step.1 = f32[128,2560]{1,0:T(8,128)S(1)} custom-call(bf16[512,2560]{1,0:T(8,128)(2,1)} %hidden_in.1, bf16[2560,128]{1,0:T(8,128)(2,1)} %head_in.1, f32[8,128]{1,0:T(8,128)} %bias_in.1, s32[1,512]{1,0:T(1,128)} %bitcast.10, s32[1,512]{1,0:T(1,128)} %bitcast.11, f32[1,512]{1,0:T(1,128)} %bitcast.12, f32[1,512]{1,0:T(1,128)} %bitcast.13, s32[1,512]{1,0:T(1,128)} %bitcast.14, ...), custom_call_target="tpu_custom_call" | custom-call | tf_op jit(solution)/shard_map/step/pallas_call | solution.py:440
  107.6 1.5 %copy.11 = f32[2560,128]{1,0:T(8,128)} copy(f32[2560,128]{0,1:T(8,128)S(1)} %bitcast.8) | data formatting | bytes 2621440 | tf_op jit(solution)/shard_map/transpose | solution.py:507

commit v4 on v3

v4 whole, which is shorter than its diff:
```python
import functools
import math

import jax
import jax.numpy as jnp
from jax import lax
from jax.experimental import pallas as pl
from jax.experimental.pallas import tpu as pltpu
from jax.sharding import PartitionSpec as P

D = 2560
A = 1024
AGENTS = 8
SEQ_LEN = 64
GAMMA = 0.99
TRACE_DECAY = 0.95
DAMPING = 0.001
RADIUS_SHARE = 0.001

MESH = pl.DeviceIdType.MESH
F32 = jnp.float32
BF16 = jnp.bfloat16
NY = 8
NZ = 4
NM = 8
ROWS = 512
SAMPLES = 2048
COLS = 128
LEFT = 1536
FAR_FIRST = (4, 3, 5, 2, 6, 1, 7)
NEAR_FIRST = (1, 7, 2, 6, 3, 5, 4)
ARRIVALS = (
    ("a", 1), ("a", 7), ("b", 1), ("a", 2), ("a", 6), ("b", 2), ("b", 3), ("a", 3), ("a", 5),
    ("a", 4),
)
CORE_ORDER = (
    ("a", 4), ("b", 3), ("a", 3), ("a", 5), ("b", 1), ("a", 2), ("a", 6), ("b", 2),
    ("a", 1), ("a", 7), ("a", 0), ("b", 0),
)


def kernel(
    hidden_in, head_in, bias_in, ids_in, actions_in, rewards_in, values_in, starts_in, ratio_in, samples_in,
    out,
    hidden, head, bias, ids, actions, rewards, values, starts, ratio, samples, loads,
    probs, lifted_grad, logit_grad, part, grad_hi, grad_lo, resid_hi,
    peak_box, centre_box, final_box, first_y, first_q, dots_m, dots_y, dots_q, adv_y, adv_q, curv_y, curv_q,
    core_a, core_b, send_a32, send_b32, y_a32, z_b32, send_a16, send_b16, y_a16, z_b16,
    own_a, own_b, z_a, y_b,
    small_s, small_r, rs_s, rs_r, rs_core, ag_s, ag_r, ag_line,
):
    dp, me_m = lax.axis_index("dp"), lax.axis_index("mp")
    core = lax.rem(dp, 2)
    y = lax.rem(dp // 2, NY)
    z = dp // (2 * NY)
    q = z * 2 + core

    def at_y(k):
        return ((z * NY + k) * 2 + core, me_m)

    def at_q(k):
        return ((k // 2 * NY + y) * 2 + lax.rem(k, 2), me_m)

    def at_z(k):
        return ((k * NY + y) * 2 + core, me_m)

    def at_m(k):
        return (dp, k)

    other = (dp + 1 - 2 * core, me_m)

    barrier = pltpu.get_barrier_semaphore()
    for o in range(1, 8):
        for target in (
            at_y(lax.rem(y + o, NY)),
            at_q(lax.rem(q + o, 8)),
            at_m(lax.rem(me_m + o, NM)),
        ):
            pl.semaphore_signal(barrier, inc=1, device_id=target, device_id_type=MESH)

    fetches = [
        pltpu.make_async_copy(src, dst, loads.at[k])
        for k, (src, dst) in enumerate(
            (
                (rewards_in, rewards), (values_in, values), (starts_in, starts),
                (hidden_in, hidden), (head_in, head), (bias_in, bias), (ids_in, ids),
                (actions_in, actions), (ratio_in, ratio), (samples_in, samples),
            )
        )
    ]
    for fetch in fetches:
        fetch.start()

    def copy(src, dst, send, recv, target):
        return pltpu.make_async_remote_copy(
            src_ref=src, dst_ref=dst, send_sem=send, recv_sem=recv,
            device_id=target, device_id_type=MESH,
        )

    def wait_sent(view, sem):
        copy(view, view, sem, sem, other).wait_send()

    def wait_come(view, sem):
        copy(view, view, sem, sem, other).wait_recv()

    def swap_start(n, box, me, place):
        for o in range(1, 8):
            copy(
                box.at[me], box.at[me], small_s.at[n], small_r.at[n], place(lax.rem(me + o, 8))
            ).start()

    def swap_wait(n, box, me, place):
        wait_come(box.at[0:7], small_r.at[n])
        wait_sent(box.at[0:7], small_s.at[n])

    def total(box):
        acc = box[0]
        for k in range(1, 8):
            acc = acc + box[k]
        return acc

    def lane_part(row):
        return row[:, 0:128] + row[:, 128:256] + row[:, 256:384] + row[:, 384:512]

    for fetch in fetches[:3]:
        fetch.wait()

    def ahead(x, s):
        return pltpu.roll(x, ROWS - s, 1)

    def wide(ref):
        return jnp.broadcast_to(ref[...].astype(F32), (8, ROWS))

    position = lax.broadcasted_iota(jnp.int32, (8, ROWS), 1)
    value = wide(values)
    ends = (lax.rem(position, SEQ_LEN) == SEQ_LEN - 1) | (ahead(wide(starts), 1) > 0.5)
    continues = jnp.where(ends, 0.0, 1.0)
    advantage = wide(rewards) + GAMMA * continues * ahead(value, 1) - value
    keeps = GAMMA * TRACE_DECAY * continues
    for s in (1, 2, 4, 8, 16, 32):
        advantage = advantage + keeps * ahead(advantage, s)
        keeps = keeps * ahead(keeps, s)
    advantage = advantage[0:1]
    adv_y[y] = lane_part(advantage)

    for fetch in fetches[3:]:
        fetch.wait()

    logits = jnp.dot(hidden[...], head[...], preferred_element_type=F32).T
    bias_t = bias[...].T
    agent = ids[...]
    for k in range(AGENTS):
        logits = logits + jnp.where(agent == k, bias_t[:, k : k + 1], 0.0)
    peak = jnp.max(logits, axis=0, keepdims=True)
    exponent = jnp.exp(logits - peak)
    peak_box[me_m, 0:1] = peak
    peak_box[me_m, 1:2] = jnp.sum(exponent, axis=0, keepdims=True)
    probs[...] = exponent
    pl.semaphore_wait(barrier, 21)
    swap_start(0, adv_y, y, at_y)
    swap_start(1, peak_box, me_m, at_m)

    local = samples[...] - dp * ROWS
    high = lax.shift_right_logical(local, 7)
    low = lax.bitwise_and(local, 127)
    high_hot = (lax.broadcasted_iota(jnp.int32, (8, SAMPLES), 0) == high).astype(F32).astype(BF16)
    low_hot = (lax.broadcasted_iota(jnp.int32, (128, SAMPLES), 0) == low).astype(F32).astype(BF16)
    tally = lax.dot_general(
        high_hot, low_hot, (((1,), (1,)), ((), ())), preferred_element_type=F32
    )
    count = jnp.concatenate([tally[0:1], tally[1:2], tally[2:3], tally[3:4]], axis=1)

    swap_wait(0, adv_y, y, at_y)
    adv_q[q] = total(adv_y)
    swap_start(2, adv_q, q, at_q)

    swap_wait(1, peak_box, me_m, at_m)
    row_peak = peak_box[0, 0:1]
    for k in range(1, NM):
        row_peak = jnp.maximum(row_peak, peak_box[k, 0:1])
    denominator = peak_box[0, 1:2] * jnp.exp(peak_box[0, 0:1] - row_peak)
    for k in range(1, NM):
        denominator = denominator + peak_box[k, 1:2] * jnp.exp(peak_box[k, 0:1] - row_peak)
    prob = probs[...] * (jnp.exp(peak - row_peak) / denominator)
    probs[...] = prob

    swap_wait(2, adv_q, q, at_q)
    tokens = ROWS * 64
    adv_mean = jnp.sum(total(adv_q), axis=1, keepdims=True) / tokens
    weight = ratio[...] * (advantage - adv_mean) / tokens
    picked = lax.broadcasted_iota(jnp.int32, (COLS, ROWS), 0) == actions[...] - me_m * COLS
    logit_grad[...] = (weight * (jnp.where(picked, 1.0, 0.0) - prob)).astype(BF16)

    def project():
        for j in range(5):
            cols = slice(512 * j, 512 * (j + 1))
            part[:, :, cols] = jnp.dot(
                logit_grad[...], hidden[:, cols], preferred_element_type=F32
            ).reshape(16, 8, 512)

    def scatter(n, send_a, send_b, y_a, z_b, between):
        def core_copy(kind, o):
            if kind == "a":
                k = (1 - core) * 8 + lax.rem(y + o, NY)
                return copy(
                    part.at[k, :, 0:LEFT], core_a.at[n, o], rs_s.at[n, 0], rs_core.at[n, o], other
                )
            k = (1 - core) * 8 + lax.rem(z + o, NZ) * 2
            return copy(
                part.at[pl.ds(k, 2), :, LEFT:D], core_b.at[n, o],
                rs_s.at[n, 1], rs_core.at[n, 8 + o], other,
            )

        for kind, o in CORE_ORDER:
            core_copy(kind, o).start()
        for kind, o in CORE_ORDER:
            core_copy(kind, o).wait_recv()
            if kind == "a":
                k = lax.rem(y + o, NY)
                term = part[core * 8 + k, :, 0:LEFT] + core_a[n, o]
                if o == 0:
                    acc_a = term
                    continue
                send_a[o] = term.astype(send_a.dtype)
                copy(send_a.at[o], y_a.at[o], rs_s.at[n, 2], rs_r.at[n, 2], at_y(k)).start()
            else:
                k = lax.rem(z + o, NZ)
                term = part[pl.ds(core * 8 + 2 * k, 2), :, LEFT:D] + core_b[n, o]
                if o == 0:
                    acc_b = term
                    continue
                send_b[o] = term.astype(send_b.dtype)
                copy(send_b.at[o], z_b.at[o], rs_s.at[n, 3], rs_r.at[n, 3], at_z(k)).start()
        wait_come(z_b.at[1:4], rs_r.at[n, 3])
        for o in (1, 2, 3):
            acc_b = acc_b + z_b[o].astype(F32)
        for k in range(NY):
            own_b[n, k] = acc_b[k // 4, :, 256 * (k % 4) : 256 * (k % 4 + 1)]
        for o in FAR_FIRST:
            k = lax.rem(y + o, NY)
            copy(own_b.at[n, k], y_b.at[n, o], rs_s.at[n, 4], rs_r.at[n, 4], at_y(k)).start()
        between()
        wait_come(y_a.at[1:8], rs_r.at[n, 2])
        for o in NEAR_FIRST:
            acc_a = acc_a + y_a[o].astype(F32)
        for k in range(NZ):
            own_a[n, k] = acc_a[:, 384 * k : 384 * (k + 1)]
        for o in (3, 2, 1):
            k = lax.rem(z + o, NZ)
            copy(own_a.at[n, k], z_a.at[n, o], rs_s.at[n, 5], rs_r.at[n, 5], at_z(k)).start()
        shard_b = own_b[n, y]
        wait_come(y_b.at[n, 1:8], rs_r.at[n, 4])
        for o in NEAR_FIRST:
            shard_b = shard_b + y_b[n, o]
        shard_a = own_a[n, z]
        wait_come(z_a.at[n, 1:4], rs_r.at[n, 5])
        for o in (1, 2, 3):
            shard_a = shard_a + z_a[n, o]
        return shard_a, shard_b

    def scatter_end(n, send_a, send_b):
        wait_sent(part.at[0:8, :, 0:LEFT], rs_s.at[n, 0])
        wait_sent(part.at[0:8, :, LEFT:D], rs_s.at[n, 1])
        wait_sent(send_a.at[1:8], rs_s.at[n, 2])
        wait_sent(send_b.at[1:4], rs_s.at[n, 3])
        wait_sent(own_b.at[n, 1:8], rs_s.at[n, 4])
        wait_sent(own_a.at[n, 1:4], rs_s.at[n, 5])

    def spot_a(full, ky, kz):
        return full.at[core * 8 + ky, :, pl.ds(pl.multiple_of(kz * 384, 128), 384)]

    def spot_b(full, ky, kz):
        columns = pl.ds(pl.multiple_of(LEFT + lax.rem(ky, 4) * 256, 128), 256)
        return full.at[core * 8 + 2 * kz + ky // 4, :, columns]

    def line_a(full, kc, ky):
        return full.at[kc * 8 + ky, :, 0:LEFT]

    def line_b(full, kc, kz):
        return full.at[pl.ds(kc * 8 + 2 * kz, 2), :, LEFT:D]

    def gather_start(n, full):
        def begin(ref, kind, recv, target):
            copy(ref, ref, ag_s.at[n, kind], recv, target).start()

        mine = core * 8 + y
        for o in (3, 2, 1):
            begin(spot_a(full, y, z), 0, ag_r.at[n, 0], at_z(lax.rem(z + o, NZ)))
        for o in FAR_FIRST:
            begin(spot_b(full, y, z), 1, ag_r.at[n, 1], at_y(lax.rem(y + o, NY)))
        wait_come(full.at[mine, :, 0 : 3 * 384], ag_r.at[n, 0])
        for o in FAR_FIRST:
            begin(line_a(full, core, y), 2, ag_line.at[n, o], at_y(lax.rem(y + o, NY)))
        begin(line_a(full, core, y), 4, ag_r.at[n, 2], other)
        wait_come(full.at[mine, :, 0 : 7 * 256], ag_r.at[n, 1])
        for o in (3, 2, 1):
            begin(line_b(full, core, z), 3, ag_line.at[n, 7 + o], at_z(lax.rem(z + o, NZ)))
        begin(line_b(full, core, z), 5, ag_r.at[n, 3], other)

    def gather_wait(n, full):
        def arrive(ref, line, kind, recv):
            wait_come(ref, ag_line.at[n, line])
            copy(ref, ref, ag_s.at[n, kind], recv, other).start()

        for kind, o in ARRIVALS:
            if kind == "a":
                arrive(line_a(full, core, lax.rem(y + NY - o, NY)), o, 4, ag_r.at[n, 2])
            else:
                arrive(line_b(full, core, lax.rem(z + NZ - o, NZ)), 7 + o, 5, ag_r.at[n, 3])
        wait_come(full.at[pl.ds((1 - core) * 8, 8), :, 0:LEFT], ag_r.at[n, 2])
        wait_come(full.at[pl.ds((1 - core) * 8, 8), :, LEFT:D], ag_r.at[n, 3])

    def gather_end(n, full):
        wait_sent(full.at[0, :, 0 : 3 * 384], ag_s.at[n, 0])
        wait_sent(full.at[0, :, 0 : 7 * 256], ag_s.at[n, 1])
        wait_sent(full.at[0:7, :, 0:LEFT], ag_s.at[n, 2])
        wait_sent(full.at[0:6, :, LEFT:D], ag_s.at[n, 3])
        wait_sent(full.at[0:8, :, 0:LEFT], ag_s.at[n, 4])
        wait_sent(full.at[0:8, :, LEFT:D], ag_s.at[n, 5])

    def keep(full, shards):
        shard_a, shard_b = shards
        full[core * 8 + y, :, pl.ds(pl.multiple_of(z * 384, 128), 384)] = shard_a.astype(BF16)
        columns = pl.ds(pl.multiple_of(LEFT + lax.rem(y, 4) * 256, 128), 256)
        full[core * 8 + 2 * z + y // 4, :, columns] = shard_b.astype(BF16)

    def lift(vector):
        return lax.dot_general(
            vector.reshape(COLS, D).astype(BF16), hidden[...], (((1,), (1,)), ((), ())),
            preferred_element_type=F32,
        )

    def folded(left, right):
        terms = [
            l[:, k : k + 128] * r[:, k : k + 128]
            for l, r in zip(left, right)
            for k in range(0, l.shape[1], 128)
        ]
        return jnp.sum(sum(terms[1:], terms[0]), axis=0, keepdims=True)

    project()
    grad_piece = scatter(0, send_a32, send_b32, y_a32, z_b32, lambda: None)
    keep(grad_hi, grad_piece)
    keep(grad_lo, [x - x.astype(BF16).astype(F32) for x in grad_piece])
    gather_start(0, grad_hi)
    gather_wait(0, grad_hi)
    scatter_end(0, send_a32, send_b32)

    def local_moments(box, prob, lifted):
        mass = jnp.sum(prob, axis=0, keepdims=True)
        moment = jnp.sum(prob * lifted, axis=0, keepdims=True)
        spread = lifted - share(moment, mass)
        box[me_m, 0:1] = moment
        box[me_m, 1:2] = jnp.sum(prob * spread * spread, axis=0, keepdims=True)

    def share(moment, mass):
        return jnp.where(mass > 0.0, moment / jnp.where(mass > 0.0, mass, 1.0), 0.0)

    def row_variance(box, centre):
        variance = jnp.zeros_like(centre)
        for k in range(NM):
            mass = peak_box[k, 1:2] * (jnp.exp(peak_box[k, 0:1] - row_peak) / denominator)
            away = share(box[k, 0:1], mass) - centre
            variance = variance + box[k, 1:2] + mass * away * away
        return variance

    lifted = lift(grad_hi[...].astype(F32))
    lifted_grad[...] = lifted
    prob = probs[...]
    local_moments(centre_box, prob, lifted)
    centre_box[me_m, 2:3] = jnp.concatenate(
        [folded(grad_piece, grad_piece), jnp.zeros((1, ROWS - 128), F32)], axis=1
    )
    swap_start(3, centre_box, me_m, at_m)
    swap_wait(3, centre_box, me_m, at_m)
    centre = total(centre_box)[0:1]
    logit_grad[...] = (count * (prob * (lifted - centre))).astype(BF16)
    first_y[y, 0:1] = lane_part(count * row_variance(centre_box, centre))
    first_y[y, 1:2] = total(centre_box)[2:3, 0:128]
    swap_start(4, first_y, y, at_y)
    project()

    def pass_on():
        swap_wait(4, first_y, y, at_y)
        first_q[q] = total(first_y)
        swap_start(5, first_q, q, at_q)

    summed = scatter(1, send_a16, send_b16, y_a16, z_b16, pass_on)
    swap_wait(5, first_q, q, at_q)
    dots = jnp.sum(total(first_q), axis=1, keepdims=True)
    rr = dots[1:2]
    curvature = dots[0:1] / (SAMPLES * 64) + DAMPING * rr
    step = rr / curvature
    quad = step * step * curvature
    resid_piece = [
        g - step * (f / (SAMPLES * 64) + DAMPING * g) for f, g in zip(summed, grad_piece)
    ]
    keep(resid_hi, resid_piece)
    dots_m[me_m] = folded(resid_piece, resid_piece)
    swap_start(6, dots_m, me_m, at_m)
    gather_start(1, resid_hi)
    swap_wait(6, dots_m, me_m, at_m)
    dots_y[y] = total(dots_m)
    swap_start(7, dots_y, y, at_y)
    swap_wait(7, dots_y, y, at_y)
    dots_q[q] = total(dots_y)
    swap_start(8, dots_q, q, at_q)
    gather_wait(1, resid_hi)

    lifted = lift(resid_hi[...].astype(F32))
    swap_wait(8, dots_q, q, at_q)
    rr_next = jnp.sum(total(dots_q), axis=1, keepdims=True)
    beta = rr_next / rr
    local_moments(final_box, probs[...], lifted + beta * lifted_grad[...])
    swap_start(9, final_box, me_m, at_m)
    gather_start(2, grad_lo)
    swap_wait(9, final_box, me_m, at_m)
    curv_y[y] = lane_part(count * row_variance(final_box, total(final_box)[0:1]))
    swap_start(10, curv_y, y, at_y)
    swap_wait(10, curv_y, y, at_y)
    curv_q[q] = total(curv_y)
    swap_start(11, curv_q, q, at_q)
    gather_wait(2, grad_lo)
    scatter_end(1, send_a16, send_b16)
    for n, full in enumerate((grad_hi, resid_hi, grad_lo)):
        gather_end(n, full)
    swap_wait(11, curv_q, q, at_q)
    curvature = jnp.sum(total(curv_q), axis=1, keepdims=True) / (SAMPLES * 64)
    curvature = curvature + DAMPING * (rr_next + beta * beta * rr)
    last = rr_next / curvature
    quad = quad + last * last * curvature
    scale = jnp.sqrt(D * A * RADIUS_SHARE / quad)
    of_grad = (step + last * beta) * scale
    of_resid = last * scale
    g = grad_hi[...].astype(F32) + grad_lo[...].astype(F32)
    out[...] = (of_grad * g + of_resid * resid_hi[...].astype(F32)).reshape(COLS, D)


def per_device(hidden, head, bias, ids, actions, rewards, values, starts, ratio, samples):
    dma = pltpu.SemaphoreType.DMA
    vmem = pltpu.VMEM

    def row(x):
        return x.reshape(1, -1)

    result = pl.pallas_call(
        kernel,
        out_shape=jax.ShapeDtypeStruct((COLS, D), F32),
        in_specs=[pl.BlockSpec(memory_space=pltpu.MemorySpace.HBM)] * 10,
        out_specs=pl.BlockSpec(memory_space=pltpu.VMEM),
        scratch_shapes=[
            vmem((ROWS, D), BF16),
            vmem((D, COLS), BF16),
            vmem((AGENTS, COLS), F32),
            vmem((1, ROWS), jnp.int32),
            vmem((1, ROWS), jnp.int32),
            vmem((1, ROWS), F32),
            vmem((1, ROWS), F32),
            vmem((1, ROWS), jnp.int32),
            vmem((1, ROWS), F32),
            vmem((1, SAMPLES), jnp.int32),
            dma((10,)),
            vmem((COLS, ROWS), F32),
            vmem((COLS, ROWS), F32),
            vmem((COLS, ROWS), BF16),
            vmem((16, 8, D), F32),
            vmem((16, 8, D), BF16),
            vmem((16, 8, D), BF16),
            vmem((16, 8, D), BF16),
            vmem((8, 2, ROWS), F32),
            vmem((8, 3, ROWS), F32),
            vmem((8, 2, ROWS), F32),
            vmem((8, 2, 128), F32),
            vmem((8, 2, 128), F32),
            vmem((8, 1, 128), F32),
            vmem((8, 1, 128), F32),
            vmem((8, 1, 128), F32),
            vmem((8, 1, 128), F32),
            vmem((8, 1, 128), F32),
            vmem((8, 1, 128), F32),
            vmem((8, 1, 128), F32),
            vmem((2, NY, 8, LEFT), F32),
            vmem((2, NZ, 2, 8, D - LEFT), F32),
            vmem((NY, 8, LEFT), F32),
            vmem((NZ, 2, 8, D - LEFT), F32),
            vmem((NY, 8, LEFT), F32),
            vmem((NZ, 2, 8, D - LEFT), F32),
            vmem((NY, 8, LEFT), BF16),
            vmem((NZ, 2, 8, D - LEFT), BF16),
            vmem((NY, 8, LEFT), BF16),
            vmem((NZ, 2, 8, D - LEFT), BF16),
            vmem((2, NZ, 8, 384), F32),
            vmem((2, NY, 8, 256), F32),
            vmem((2, NZ, 8, 384), F32),
            vmem((2, NY, 8, 256), F32),
            dma((12,)),
            dma((12,)),
            dma((2, 6)),
            dma((2, 6)),
            dma((2, 12)),
            dma((3, 6)),
            dma((3, 4)),
            dma((3, 11)),
        ],
        compiler_params=pltpu.CompilerParams(
            collective_id=0, has_side_effects=True, vmem_limit_bytes=40 * 1024 * 1024
        ),
        name="step",
    )(
        *(
            pltpu.with_memory_space_constraint(x, pltpu.MemorySpace.HBM)
            for x in (
                hidden, head, bias, row(ids), row(actions), row(rewards), row(values), row(starts),
                row(ratio), row(samples),
            )
        )
    )
    return result.T


def solution(mesh):
    placed = (P("dp", None), P(None, "mp"), P(None, "mp")) + (P("dp"),) * 7
    return jax.shard_map(
        per_device, mesh=mesh, in_specs=placed, out_specs=P(None, "mp"), check_vma=False
    )
```

time: 109 us -> 103 us (0.945)
  Pallas kernels: 108 us -> 102 us
    pallas_call x1, Pallas kernels: 108 us -> 102 us  [per_device(): pl.pallas_call(kernel, out_shape=jax.ShapeDtypeStruct((COLS, D), F32), in...]
where the time goes in v4:
time: 103 us
  Pallas kernels  102 us (99%)
  local copies, waits for them, and re-layouts  1.46 us (1%)
    pallas_call x1, Pallas kernels, per_device(): pl.pallas_call(kernel, out_shape=jax.ShapeDtypeStruct((COLS, D), F32), in...  102 us

profile of v4, /device:TPU:1, one launch (start us, length us, event | category | flops | bytes accessed | tf_op | source)
XLA Modules:
  0.0 103.2 jit_solution(425723741768504319)
XLA Ops:
  0.0 101.8 %step.1 = f32[128,2560]{1,0:T(8,128)S(1)} custom-call(bf16[512,2560]{1,0:T(8,128)(2,1)} %hidden_in.1, bf16[2560,128]{1,0:T(8,128)(2,1)} %head_in.1, f32[8,128]{1,0:T(8,128)} %bias_in.1, s32[1,512]{1,0:T(1,128)} %bitcast.10, s32[1,512]{1,0:T(1,128)} %bitcast.11, f32[1,512]{1,0:T(1,128)} %bitcast.12, f32[1,512]{1,0:T(1,128)} %bitcast.13, s32[1,512]{1,0:T(1,128)} %bitcast.14, ...), custom_call_target="tpu_custom_call" | custom-call | tf_op jit(solution)/shard_map/step/pallas_call | solution.py:446
  101.8 1.5 %copy.11 = f32[2560,128]{1,0:T(8,128)} copy(f32[2560,128]{0,1:T(8,128)S(1)} %bitcast.8) | data formatting | bytes 2621440 | tf_op jit(solution)/shard_map/transpose | solution.py:518

commit v5 on v4

--- a/solution.py
+++ b/solution.py
@@ -43,7 +43,7 @@
     hidden_in, head_in, bias_in, ids_in, actions_in, rewards_in, values_in, starts_in, ratio_in, samples_in,
     out,
     hidden, head, bias, ids, actions, rewards, values, starts, ratio, samples, loads,
-    probs, lifted_grad, logit_grad, part, grad_hi, grad_lo, resid_hi,
+    probs, weighted_spread, logit_grad, grad_t, resid_t, part, grad_hi, grad_lo, resid_hi,
     peak_box, centre_box, final_box, first_y, first_q, dots_m, dots_y, dots_q, adv_y, adv_q, curv_y, curv_q,
     core_a, core_b, send_a32, send_b32, y_a32, z_b32, send_a16, send_b16, y_a16, z_b16,
     own_a, own_b, z_a, y_b,
@@ -191,8 +191,8 @@
     picked = lax.broadcasted_iota(jnp.int32, (COLS, ROWS), 0) == actions[...] - me_m * COLS
     logit_grad[...] = (weight * (jnp.where(picked, 1.0, 0.0) - prob)).astype(BF16)
 
-    def project():
-        for j in range(5):
+    def project(tiles):
+        for j in tiles:
             cols = slice(512 * j, 512 * (j + 1))
             part[:, :, cols] = jnp.dot(
                 logit_grad[...], hidden[:, cols], preferred_element_type=F32
@@ -211,8 +211,11 @@
                 rs_s.at[n, 1], rs_core.at[n, 8 + o], other,
             )
 
-        for kind, o in CORE_ORDER:
-            core_copy(kind, o).start()
+        for tiles, part_kind in ((range(3), "a"), (range(3, 5), "b")):
+            project(tiles)
+            for kind, o in CORE_ORDER:
+                if kind == part_kind:
+                    core_copy(kind, o).start()
         for kind, o in CORE_ORDER:
             core_copy(kind, o).wait_recv()
             if kind == "a":
@@ -338,7 +341,6 @@
         ]
         return jnp.sum(sum(terms[1:], terms[0]), axis=0, keepdims=True)
 
-    project()
     grad_piece = scatter(0, send_a32, send_b32, y_a32, z_b32, lambda: None)
     keep(grad_hi, grad_piece)
     keep(grad_lo, [x - x.astype(BF16).astype(F32) for x in grad_piece])
@@ -352,22 +354,28 @@
         spread = lifted - share(moment, mass)
         box[me_m, 0:1] = moment
         box[me_m, 1:2] = jnp.sum(prob * spread * spread, axis=0, keepdims=True)
+        return spread
 
     def share(moment, mass):
         return jnp.where(mass > 0.0, moment / jnp.where(mass > 0.0, mass, 1.0), 0.0)
 
-    def row_variance(box, centre):
-        variance = jnp.zeros_like(centre)
-        for k in range(NM):
-            mass = peak_box[k, 1:2] * (jnp.exp(peak_box[k, 0:1] - row_peak) / denominator)
-            away = share(box[k, 0:1], mass) - centre
-            variance = variance + box[k, 1:2] + mass * away * away
-        return variance
+    def row_aways(box):
+        masses = [
+            peak_box[k, 1:2] * (jnp.exp(peak_box[k, 0:1] - row_peak) / denominator)
+            for k in range(NM)
+        ]
+        centre = total(box)[0:1]
+        return masses, [share(box[k, 0:1], m) - centre for k, m in enumerate(masses)]
+
+    def row_sum(box, row, masses, left, right):
+        acc = total(box)[row : row + 1]
+        for m, l, r in zip(masses, left, right):
+            acc = acc + m * l * r
+        return acc
 
     lifted = lift(grad_hi[...].astype(F32))
-    lifted_grad[...] = lifted
     prob = probs[...]
-    local_moments(centre_box, prob, lifted)
+    weighted_spread[...] = prob * local_moments(centre_box, prob, lifted)
     centre_box[me_m, 2:3] = jnp.concatenate(
         [folded(grad_piece, grad_piece), jnp.zeros((1, ROWS - 128), F32)], axis=1
     )
@@ -375,10 +383,10 @@
     swap_wait(3, centre_box, me_m, at_m)
     centre = total(centre_box)[0:1]
     logit_grad[...] = (count * (prob * (lifted - centre))).astype(BF16)
-    first_y[y, 0:1] = lane_part(count * row_variance(centre_box, centre))
+    masses, aways = row_aways(centre_box)
+    first_y[y, 0:1] = lane_part(count * row_sum(centre_box, 1, masses, aways, aways))
     first_y[y, 1:2] = total(centre_box)[2:3, 0:128]
     swap_start(4, first_y, y, at_y)
-    project()
 
     def pass_on():
         swap_wait(4, first_y, y, at_y)
@@ -403,20 +411,23 @@
     dots_y[y] = total(dots_m)
     swap_start(7, dots_y, y, at_y)
     swap_wait(7, dots_y, y, at_y)
+    gather_wait(1, resid_hi)
+
+    lifted = lift(resid_hi[...].astype(F32))
+    spread = local_moments(final_box, probs[...], lifted)
+    final_box[me_m, 2:3] = jnp.sum(weighted_spread[...] * spread, axis=0, keepdims=True)
+    swap_start(9, final_box, me_m, at_m)
     dots_q[q] = total(dots_y)
     swap_start(8, dots_q, q, at_q)
-    gather_wait(1, resid_hi)
-
-    lifted = lift(resid_hi[...].astype(F32))
+    gather_start(2, grad_lo)
+    swap_wait(9, final_box, me_m, at_m)
+    _, resid_aways = row_aways(final_box)
+    curv_y[y, 0:1] = lane_part(count * row_sum(final_box, 1, masses, resid_aways, resid_aways))
+    curv_y[y, 1:2] = lane_part(count * row_sum(final_box, 2, masses, resid_aways, aways))
+    swap_start(10, curv_y, y, at_y)
     swap_wait(8, dots_q, q, at_q)
     rr_next = jnp.sum(total(dots_q), axis=1, keepdims=True)
     beta = rr_next / rr
-    local_moments(final_box, probs[...], lifted + beta * lifted_grad[...])
-    swap_start(9, final_box, me_m, at_m)
-    gather_start(2, grad_lo)
-    swap_wait(9, final_box, me_m, at_m)
-    curv_y[y] = lane_part(count * row_variance(final_box, total(final_box)[0:1]))
-    swap_start(10, curv_y, y, at_y)
     swap_wait(10, curv_y, y, at_y)
     curv_q[q] = total(curv_y)
     swap_start(11, curv_q, q, at_q)
@@ -424,16 +435,23 @@
     scatter_end(1, send_a16, send_b16)
     for n, full in enumerate((grad_hi, resid_hi, grad_lo)):
         gather_end(n, full)
+    for k in range(16):
+        part[k] = grad_hi[k].astype(F32) + grad_lo[k].astype(F32)
+    for j in range(D // 128):
+        cols = slice(128 * j, 128 * (j + 1))
+        grad_t[cols] = part[:, :, cols].reshape(COLS, 128).T
+        resid_t[cols] = resid_hi[:, :, cols].astype(F32).reshape(COLS, 128).T
     swap_wait(11, curv_q, q, at_q)
-    curvature = jnp.sum(total(curv_q), axis=1, keepdims=True) / (SAMPLES * 64)
+    curves = jnp.sum(total(curv_q), axis=1, keepdims=True)
+    curvature = curves[0:1] + 2.0 * beta * curves[1:2] + beta * beta * dots[0:1]
+    curvature = curvature / (SAMPLES * 64)
     curvature = curvature + DAMPING * (rr_next + beta * beta * rr)
     last = rr_next / curvature
     quad = quad + last * last * curvature
     scale = jnp.sqrt(D * A * RADIUS_SHARE / quad)
     of_grad = (step + last * beta) * scale
     of_resid = last * scale
-    g = grad_hi[...].astype(F32) + grad_lo[...].astype(F32)
-    out[...] = (of_grad * g + of_resid * resid_hi[...].astype(F32)).reshape(COLS, D)
+    out[...] = of_grad * grad_t[...] + of_resid * resid_t[...]
 
 
 def per_device(hidden, head, bias, ids, actions, rewards, values, starts, ratio, samples):
@@ -443,9 +461,9 @@
     def row(x):
         return x.reshape(1, -1)
 
-    result = pl.pallas_call(
+    return pl.pallas_call(
         kernel,
-        out_shape=jax.ShapeDtypeStruct((COLS, D), F32),
+        out_shape=jax.ShapeDtypeStruct((D, COLS), F32),
         in_specs=[pl.BlockSpec(memory_space=pltpu.MemorySpace.HBM)] * 10,
         out_specs=pl.BlockSpec(memory_space=pltpu.VMEM),
         scratch_shapes=[
@@ -463,13 +481,15 @@
             vmem((COLS, ROWS), F32),
             vmem((COLS, ROWS), F32),
             vmem((COLS, ROWS), BF16),
+            vmem((D, COLS), F32),
+            vmem((D, COLS), F32),
             vmem((16, 8, D), F32),
             vmem((16, 8, D), BF16),
             vmem((16, 8, D), BF16),
             vmem((16, 8, D), BF16),
             vmem((8, 2, ROWS), F32),
             vmem((8, 3, ROWS), F32),
-            vmem((8, 2, ROWS), F32),
+            vmem((8, 3, ROWS), F32),
             vmem((8, 2, 128), F32),
             vmem((8, 2, 128), F32),
             vmem((8, 1, 128), F32),
@@ -477,8 +497,8 @@
             vmem((8, 1, 128), F32),
             vmem((8, 1, 128), F32),
             vmem((8, 1, 128), F32),
-            vmem((8, 1, 128), F32),
-            vmem((8, 1, 128), F32),
+            vmem((8, 2, 128), F32),
+            vmem((8, 2, 128), F32),
             vmem((2, NY, 8, LEFT), F32),
             vmem((2, NZ, 2, 8, D - LEFT), F32),
             vmem((NY, 8, LEFT), F32),
@@ -515,7 +535,6 @@
             )
         )
     )
-    return result.T
 
 
 def solution(mesh):

time: 103 us -> 100 us (0.971)
  Pallas kernels: 102 us -> 99 us
    pallas_call x1, Pallas kernels: 102 us -> 99 us  [per_device(): pl.pallas_call(kernel, out_shape=jax.ShapeDtypeStruct((D, COLS), F32), in...]
    transpose x1 -> x0, local copies, waits for them, and re-layouts: 1.46 us -> none  [per_device(): return result.T]
    unnamed x0 -> x1, local copies, waits for them, and re-layouts: none -> 1.06 us
where the time goes in v5:
time: 100 us
  Pallas kernels  99 us (99%)
  local copies, waits for them, and re-layouts  1.06 us (1%)
    pallas_call x1, Pallas kernels, per_device(): pl.pallas_call(kernel, out_shape=jax.ShapeDtypeStruct((D, COLS), F32), in...  99 us

profile of v5, /device:TPU:1, one launch (start us, length us, event | category | flops | bytes accessed | tf_op | source)
XLA Modules:
  0.0 100.1 jit_solution(1753643267039561108)
XLA Ops:
  0.0 99.0 %step.1 = f32[2560,128]{1,0:T(8,128)S(1)} custom-call(bf16[512,2560]{1,0:T(8,128)(2,1)} %hidden_in.1, bf16[2560,128]{1,0:T(8,128)(2,1)} %head_in.1, f32[8,128]{1,0:T(8,128)} %bias_in.1, s32[1,512]{1,0:T(1,128)} %bitcast.8, s32[1,512]{1,0:T(1,128)} %bitcast.9, f32[1,512]{1,0:T(1,128)} %bitcast.10, f32[1,512]{1,0:T(1,128)} %bitcast.11, s32[1,512]{1,0:T(1,128)} %bitcast.12, ...), custom_call_target="tpu_custom_call" | custom-call | tf_op jit(solution)/shard_map/step/pallas_call | solution.py:464
  99.0 1.1 %copy.12 = f32[2560,128]{1,0:T(8,128)} copy(f32[2560,128]{1,0:T(8,128)S(1)} %step.1) | data formatting | bytes 2621440

commit v6 on v5

--- a/solution.py
+++ b/solution.py
@@ -45,8 +45,9 @@
     hidden, head, bias, ids, actions, rewards, values, starts, ratio, samples, loads,
     probs, weighted_spread, logit_grad, grad_t, resid_t, part, grad_hi, grad_lo, resid_hi,
     peak_box, centre_box, final_box, first_y, first_q, dots_m, dots_y, dots_q, adv_y, adv_q, curv_y, curv_q,
-    core_a, core_b, send_a32, send_b32, y_a32, z_b32, send_a16, send_b16, y_a16, z_b16,
+    core_a, core_b, send_a0, send_b0, y_a0, z_b0, send_a1, send_b1, y_a1, z_b1,
     own_a, own_b, z_a, y_b,
+    rest_a, rest_b, rest_y, rest_z, rest_own_a, rest_own_b, rest_za, rest_yb, rest_s, rest_r,
     small_s, small_r, rs_s, rs_r, rs_core, ag_s, ag_r, ag_line,
 ):
     dp, me_m = lax.axis_index("dp"), lax.axis_index("mp")
@@ -198,7 +199,7 @@
                 logit_grad[...], hidden[:, cols], preferred_element_type=F32
             ).reshape(16, 8, 512)
 
-    def scatter(n, send_a, send_b, y_a, z_b, between):
+    def scatter(n, send_a, send_b, y_a, z_b, between, then):
         def core_copy(kind, o):
             if kind == "a":
                 k = (1 - core) * 8 + lax.rem(y + o, NY)
@@ -224,7 +225,9 @@
                 if o == 0:
                     acc_a = term
                     continue
-                send_a[o] = term.astype(send_a.dtype)
+                send_a[o] = term.astype(BF16)
+                if n == 0:
+                    rest_a[o] = (term - term.astype(BF16).astype(F32)).astype(BF16)
                 copy(send_a.at[o], y_a.at[o], rs_s.at[n, 2], rs_r.at[n, 2], at_y(k)).start()
             else:
                 k = lax.rem(z + o, NZ)
@@ -232,7 +235,9 @@
                 if o == 0:
                     acc_b = term
                     continue
-                send_b[o] = term.astype(send_b.dtype)
+                send_b[o] = term.astype(BF16)
+                if n == 0:
+                    rest_b[o] = (term - term.astype(BF16).astype(F32)).astype(BF16)
                 copy(send_b.at[o], z_b.at[o], rs_s.at[n, 3], rs_r.at[n, 3], at_z(k)).start()
         wait_come(z_b.at[1:4], rs_r.at[n, 3])
         for o in (1, 2, 3):
@@ -251,6 +256,7 @@
         for o in (3, 2, 1):
             k = lax.rem(z + o, NZ)
             copy(own_a.at[n, k], z_a.at[n, o], rs_s.at[n, 5], rs_r.at[n, 5], at_z(k)).start()
+        then()
         shard_b = own_b[n, y]
         wait_come(y_b.at[n, 1:8], rs_r.at[n, 4])
         for o in NEAR_FIRST:
@@ -260,6 +266,50 @@
         for o in (1, 2, 3):
             shard_a = shard_a + z_a[n, o]
         return shard_a, shard_b
+
+    def rest_start():
+        for o in FAR_FIRST:
+            copy(
+                rest_a.at[o], rest_y.at[o], rest_s.at[0], rest_r.at[0], at_y(lax.rem(y + o, NY))
+            ).start()
+        for o in (3, 2, 1):
+            copy(
+                rest_b.at[o], rest_z.at[o], rest_s.at[1], rest_r.at[1], at_z(lax.rem(z + o, NZ))
+            ).start()
+
+    def rest_turn():
+        wait_come(rest_z.at[1:4], rest_r.at[1])
+        acc = rest_z[1].astype(F32) + rest_z[2].astype(F32) + rest_z[3].astype(F32)
+        for k in range(NY):
+            cols = slice(256 * (k % 4), 256 * (k % 4 + 1))
+            rest_own_b[k] = acc[k // 4, :, cols].astype(BF16)
+        for o in FAR_FIRST:
+            k = lax.rem(y + o, NY)
+            copy(rest_own_b.at[k], rest_yb.at[o], rest_s.at[2], rest_r.at[2], at_y(k)).start()
+        wait_come(rest_y.at[1:8], rest_r.at[0])
+        acc = rest_y[1].astype(F32)
+        for o in range(2, 8):
+            acc = acc + rest_y[o].astype(F32)
+        for k in range(NZ):
+            rest_own_a[k] = acc[:, 384 * k : 384 * (k + 1)].astype(BF16)
+        for o in (3, 2, 1):
+            k = lax.rem(z + o, NZ)
+            copy(rest_own_a.at[k], rest_za.at[o], rest_s.at[3], rest_r.at[3], at_z(k)).start()
+
+    def rest_wait():
+        rest_of_b = rest_own_b[y].astype(F32)
+        wait_come(rest_yb.at[1:8], rest_r.at[2])
+        for o in range(1, 8):
+            rest_of_b = rest_of_b + rest_yb[o].astype(F32)
+        rest_of_a = rest_own_a[z].astype(F32)
+        wait_come(rest_za.at[1:4], rest_r.at[3])
+        for o in range(1, 4):
+            rest_of_a = rest_of_a + rest_za[o].astype(F32)
+        wait_sent(rest_a.at[1:8], rest_s.at[0])
+        wait_sent(rest_b.at[1:4], rest_s.at[1])
+        wait_sent(rest_own_b.at[1:8], rest_s.at[2])
+        wait_sent(rest_own_a.at[1:4], rest_s.at[3])
+        return rest_of_a, rest_of_b
 
     def scatter_end(n, send_a, send_b):
         wait_sent(part.at[0:8, :, 0:LEFT], rs_s.at[n, 0])
@@ -341,12 +391,14 @@
         ]
         return jnp.sum(sum(terms[1:], terms[0]), axis=0, keepdims=True)
 
-    grad_piece = scatter(0, send_a32, send_b32, y_a32, z_b32, lambda: None)
-    keep(grad_hi, grad_piece)
-    keep(grad_lo, [x - x.astype(BF16).astype(F32) for x in grad_piece])
+    grad_first = scatter(0, send_a0, send_b0, y_a0, z_b0, lambda: None, rest_start)
+    keep(grad_hi, grad_first)
     gather_start(0, grad_hi)
+    rest_turn()
     gather_wait(0, grad_hi)
-    scatter_end(0, send_a32, send_b32)
+    scatter_end(0, send_a0, send_b0)
+    grad_piece = [x + r for x, r in zip(grad_first, rest_wait())]
+    keep(grad_lo, [x - f.astype(BF16).astype(F32) for x, f in zip(grad_piece, grad_first)])
 
     def local_moments(box, prob, lifted):
         mass = jnp.sum(prob, axis=0, keepdims=True)
@@ -393,7 +445,7 @@
         first_q[q] = total(first_y)
         swap_start(5, first_q, q, at_q)
 
-    summed = scatter(1, send_a16, send_b16, y_a16, z_b16, pass_on)
+    summed = scatter(1, send_a1, send_b1, y_a1, z_b1, pass_on, lambda: None)
     swap_wait(5, first_q, q, at_q)
     dots = jnp.sum(total(first_q), axis=1, keepdims=True)
     rr = dots[1:2]
@@ -432,7 +484,7 @@
     curv_q[q] = total(curv_y)
     swap_start(11, curv_q, q, at_q)
     gather_wait(2, grad_lo)
-    scatter_end(1, send_a16, send_b16)
+    scatter_end(1, send_a1, send_b1)
     for n, full in enumerate((grad_hi, resid_hi, grad_lo)):
         gather_end(n, full)
     for k in range(16):
@@ -501,10 +553,10 @@
             vmem((8, 2, 128), F32),
             vmem((2, NY, 8, LEFT), F32),
             vmem((2, NZ, 2, 8, D - LEFT), F32),
-            vmem((NY, 8, LEFT), F32),
-            vmem((NZ, 2, 8, D - LEFT), F32),
-            vmem((NY, 8, LEFT), F32),
-            vmem((NZ, 2, 8, D - LEFT), F32),
+            vmem((NY, 8, LEFT), BF16),
+            vmem((NZ, 2, 8, D - LEFT), BF16),
+            vmem((NY, 8, LEFT), BF16),
+            vmem((NZ, 2, 8, D - LEFT), BF16),
             vmem((NY, 8, LEFT), BF16),
             vmem((NZ, 2, 8, D - LEFT), BF16),
             vmem((NY, 8, LEFT), BF16),
@@ -513,6 +565,16 @@
             vmem((2, NY, 8, 256), F32),
             vmem((2, NZ, 8, 384), F32),
             vmem((2, NY, 8, 256), F32),
+            vmem((NY, 8, LEFT), BF16),
+            vmem((NZ, 2, 8, D - LEFT), BF16),
+            vmem((NY, 8, LEFT), BF16),
+            vmem((NZ, 2, 8, D - LEFT), BF16),
+            vmem((NZ, 8, 384), BF16),
+            vmem((NY, 8, 256), BF16),
+            vmem((NZ, 8, 384), BF16),
+            vmem((NY, 8, 256), BF16),
+            dma((4,)),
+            dma((4,)),
             dma((12,)),
             dma((12,)),
             dma((2, 6)),

time: 100 us -> 98 us (0.980)
  Pallas kernels: 99 us -> 96.8 us
    pallas_call x1, Pallas kernels: 99 us -> 96.8 us  [per_device(): pl.pallas_call(kernel, out_shape=jax.ShapeDtypeStruct((D, COLS), F32), in...]
where the time goes in v6:
time: 98 us; the launch traced here: 97.9 us
  Pallas kernels  96.8 us (99%)
  local copies, waits for them, and re-layouts  1.06 us (1%)
    pallas_call x1, Pallas kernels, per_device(): pl.pallas_call(kernel, out_shape=jax.ShapeDtypeStruct((D, COLS), F32), in...  96.8 us

profile of v6, /device:TPU:1, one launch (start us, length us, event | category | flops | bytes accessed | tf_op | source)
XLA Modules:
  0.0 97.9 jit_solution(16465078584587992215)
XLA Ops:
  0.0 96.8 %step.1 = f32[2560,128]{1,0:T(8,128)S(1)} custom-call(bf16[512,2560]{1,0:T(8,128)(2,1)} %hidden_in.1, bf16[2560,128]{1,0:T(8,128)(2,1)} %head_in.1, f32[8,128]{1,0:T(8,128)} %bias_in.1, s32[1,512]{1,0:T(1,128)} %bitcast.8, s32[1,512]{1,0:T(1,128)} %bitcast.9, f32[1,512]{1,0:T(1,128)} %bitcast.10, f32[1,512]{1,0:T(1,128)} %bitcast.11, s32[1,512]{1,0:T(1,128)} %bitcast.12, ...), custom_call_target="tpu_custom_call" | custom-call | tf_op jit(solution)/shard_map/step/pallas_call | solution.py:516
  96.8 1.1 %copy.12 = f32[2560,128]{1,0:T(8,128)} copy(f32[2560,128]{1,0:T(8,128)S(1)} %step.1) | data formatting | bytes 2621440

commit v7 on v6

--- a/solution.py
+++ b/solution.py
@@ -432,6 +432,7 @@
         [folded(grad_piece, grad_piece), jnp.zeros((1, ROWS - 128), F32)], axis=1
     )
     swap_start(3, centre_box, me_m, at_m)
+    gather_start(2, grad_lo)
     swap_wait(3, centre_box, me_m, at_m)
     centre = total(centre_box)[0:1]
     logit_grad[...] = (count * (prob * (lifted - centre))).astype(BF16)
@@ -471,7 +472,6 @@
     swap_start(9, final_box, me_m, at_m)
     dots_q[q] = total(dots_y)
     swap_start(8, dots_q, q, at_q)
-    gather_start(2, grad_lo)
     swap_wait(9, final_box, me_m, at_m)
     _, resid_aways = row_aways(final_box)
     curv_y[y, 0:1] = lane_part(count * row_sum(final_box, 1, masses, resid_aways, resid_aways))

time: 98 us -> 96.9 us (0.989)
  Pallas kernels: 96.8 us -> 95.7 us
    pallas_call x1, Pallas kernels: 96.8 us -> 95.7 us  [per_device(): pl.pallas_call(kernel, out_shape=jax.ShapeDtypeStruct((D, COLS), F32), in...]
where the time goes in v7:
time: 96.9 us; the launch traced here: 96.8 us
  Pallas kernels  95.7 us (99%)
  local copies, waits for them, and re-layouts  1.06 us (1%)
    pallas_call x1, Pallas kernels, per_device(): pl.pallas_call(kernel, out_shape=jax.ShapeDtypeStruct((D, COLS), F32), in...  95.7 us

profile of v7, /device:TPU:1, one launch (start us, length us, event | category | flops | bytes accessed | tf_op | source)
XLA Modules:
  0.0 96.8 jit_solution(3886847866979919884)
XLA Ops:
  0.0 95.7 %step.1 = f32[2560,128]{1,0:T(8,128)S(1)} custom-call(bf16[512,2560]{1,0:T(8,128)(2,1)} %hidden_in.1, bf16[2560,128]{1,0:T(8,128)(2,1)} %head_in.1, f32[8,128]{1,0:T(8,128)} %bias_in.1, s32[1,512]{1,0:T(1,128)} %bitcast.8, s32[1,512]{1,0:T(1,128)} %bitcast.9, f32[1,512]{1,0:T(1,128)} %bitcast.10, f32[1,512]{1,0:T(1,128)} %bitcast.11, s32[1,512]{1,0:T(1,128)} %bitcast.12, ...), custom_call_target="tpu_custom_call" | custom-call | tf_op jit(solution)/shard_map/step/pallas_call | solution.py:516
  95.7 1.1 %copy.12 = f32[2560,128]{1,0:T(8,128)} copy(f32[2560,128]{1,0:T(8,128)S(1)} %step.1) | data formatting | bytes 2621440
